TPU v7x, 128 devices: a whole 4x4x4 slice. The times are simulated.
128 devices in a mesh: elem: 16 (over z_hi, y, core), mode: 8 (over x, z_lo).
Axes of the slice: x: 4, y: 4, z: 4 (z_hi: 2, z_lo: 2; z = z_hi * 2 + z_lo), core: 2. Of those that a mesh axis runs over, the one named last changes fastest.
Arguments:
- iterate: float32 [480, 16384], P('mode', 'elem'), may hold values from -0.75 to 0.75
- newton_residual: float32 [480, 16384], P('mode', 'elem'), may hold values from -6 to 6
- inverse_blocks: float32 [64, 16384], P(None, 'elem'), may hold values from -0.15 to 2
- basis_values: bfloat16 [1024, 480], replicated, may hold values from -4 to 4, as said below
- triple_blocks: bfloat16 [8, 60, 20160], P('mode', None, 'elem'), may hold values from -0.375 to 0.375
- block_columns: int32 [8, 4], P('mode'), may hold values from 0 to 7, as said below
- neighbour_ids: int32 [256, 6], P('elem'), may hold values from 0 to 15, as said below
Outputs:
- correction: float32 [480, 16384], P('mode', 'elem')
- linear_residual: float32 [480, 16384], P('mode', 'elem')
Inputs may be any that keep to these rules, and one draw needn't show every extreme that they name: `neighbour_ids`: columns 0 to 3 give the neighbour across the -y, +y, -z, +z faces within the element's own block of 16 elements; columns 4 and 5 the neighbour across the -x and +x faces within the previous and the next block, cyclically. Neighbours are mutual across opposite faces. `block_columns`: row b names 4 different block columns; the first is b. `basis_values`: column 0 holds ones, the constant mode.
All inputs are finite; a program needn't handle non-finite values.
Results may differ from a plain program's by a relative error of at most 0.0039.
Values may be sent and summed in bfloat16 or wider, within the bound.
No kernel may reach another device: no remote copies, remote signals or barrier semaphores. Data moves between devices by JAX's collectives and lax.ppermute only.
A program may use at most 128 MiB of HBM per device.

v0:
```python
import math

import jax
import jax.numpy as jnp
import numpy as np
from jax import lax
from jax.experimental import pallas as pl
from jax.experimental.pallas import tpu as pltpu
from jax.sharding import PartitionSpec as P

K = 84
S = 1024
ITERS = 2
MB = 60
ROWS = 64
NODES = 1024
PAIRS = 42
GROWTH = 0.5
TIME_STEP = 0.03
LIFT_SCALE = 6.0
PENALTY = 3.0
RELAX_WEIGHT = 0.8
FACE_OPPOSITE = (1, 0, 3, 2, 5, 4)
BF = jnp.bfloat16
F32 = jnp.float32
VMEM = pl.BlockSpec(memory_space=pltpu.VMEM)
SMEM = pl.BlockSpec(memory_space=pltpu.SMEM)
ANY = pl.BlockSpec(memory_space=pl.ANY)


def line_derivative():
    inward = 1.0 / math.sqrt(5.0)
    points = np.array([-1.0, -inward, inward, 1.0])
    legendre = (5.0 * points**3 - 3.0 * points) / 2.0
    matrix = np.zeros((4, 4))
    for source in range(4):
        for target in range(4):
            if source != target:
                matrix[source, target] = legendre[source] / (
                    legendre[target] * (points[source] - points[target])
                )
    matrix[0, 0] = -3.0
    matrix[3, 3] = 3.0
    return matrix


def direction_tables():
    line_matrix = line_derivative()
    identity = np.eye(4)
    singles = [
        np.kron(np.kron(line_matrix, identity), identity),
        np.kron(np.kron(identity, line_matrix), identity),
        np.kron(np.kron(identity, identity), line_matrix),
    ]
    return [np.kron(np.eye(2), single).T.astype(np.float32) for single in singles]


def face_nodes():
    layout = np.arange(64).reshape(4, 4, 4)
    return [
        layout[:, 0, :].ravel(),
        layout[:, 3, :].ravel(),
        layout[:, :, 0].ravel(),
        layout[:, :, 3].ravel(),
        layout[0].ravel(),
        layout[3].ravel(),
    ]


def two_parts(table):
    high = np.asarray(table, np.float32).astype(jnp.bfloat16)
    low = (np.asarray(table, np.float32) - high.astype(np.float32)).astype(jnp.bfloat16)
    return high, low


def gradient_table():
    high, low = two_parts(np.concatenate(direction_tables(), axis=1))
    return np.concatenate([high, low], axis=0)


def own_tables():
    tables = direction_tables()
    nodes = face_nodes()
    result = []
    for axis, faces in enumerate(((4, 5), (0, 1), (2, 3))):
        table = tables[axis].copy()
        for sign, face in zip((-1.0, 1.0), faces):
            for node in nodes[face]:
                for half in (0, 64):
                    table[half + node, half + node] -= 0.5 * LIFT_SCALE * sign
        result.append(table)
    high, low = two_parts(np.concatenate(result, axis=0))
    return np.stack([high, low])


def near_table():
    nodes = face_nodes()
    table = np.zeros((256, 128), np.float32)
    for face in range(4):
        for source, target in zip(nodes[FACE_OPPOSITE[face]], nodes[face]):
            table[64 * face + source, target] = 1.0
            table[64 * face + source, 64 + target] = 1.0
    return table.astype(jnp.bfloat16)


def trace_table():
    table = np.zeros((2, 512, 128), np.float32)
    for element in range(8):
        for node in range(16):
            table[0, 64 * element + node, 16 * element + node] = 1.0
            table[1, 64 * element + 48 + node, 16 * element + node] = 1.0
    return table.astype(jnp.bfloat16)


def face_count():
    count = np.zeros((1, 128), np.float32)
    for nodes in face_nodes():
        for node in nodes:
            count[0, node] += 1.0
            count[0, 64 + node] += 1.0
    return count


def dot(left, right):
    return jnp.dot(left, right, preferred_element_type=F32)


def split(value):
    high = value.astype(BF)
    return high, (value - high.astype(F32)).astype(BF)


def call(body, outs, ins, scratch=(), limit=56 << 20):
    specs = [VMEM if isinstance(o, jax.ShapeDtypeStruct) else o for o in outs]
    return pl.pallas_call(
        body,
        out_shape=tuple(outs),
        in_specs=list(ins),
        out_specs=tuple(specs),
        scratch_shapes=list(scratch),
        compiler_params=pltpu.CompilerParams(vmem_limit_bytes=limit),
    )


def stored_body(x_ref, z_ref, wide, tall):
    wide[...] = jnp.zeros_like(wide)
    x = x_ref[...].astype(F32)
    wide[0:60, 0:1260] = x
    wide[64:124, 0:1259] = x[:, 1:]
    for block in range(10):
        tall[128 * block : 128 * block + 128, :] = wide[:, 128 * block : 128 * block + 128].T
    tall[1280:1344, :] = jnp.zeros((64, 128), F32)
    for pair in range(PAIRS):
        z_ref[pair] = tall[pl.ds(2 * pair, 16, stride=K), :].astype(BF)


def turn_body(side_ref, held, eye_ref, tt_ref):
    side = side_ref[0]

    def step(twin, carry):
        rows = []
        for place in range(8):
            zone = side if place < 4 else 1 - side
            rows.append(held[place % 4, zone, pl.ds(2 * twin, 2)])
        both = jnp.concatenate([row[pair] for pair in range(2) for row in rows], axis=0)
        turned = lax.dot_general(
            eye_ref[...], both, (((1,), (1,)), ((), ())), preferred_element_type=F32
        ).astype(BF)
        for pair in range(2):
            for half in range(2):
                for tile in range(4):
                    first = 64 * half + 16 * tile
                    tt_ref[tile, 4 * twin + 2 * pair + half] = turned[
                        first : first + 16, 128 * pair : 128 * pair + 128
                    ]
        return carry

    lax.fori_loop(0, PAIRS // 2, step, 0, unroll=3)


def coefficient_body(spot_ref, *refs):
    pieces, basis_ref, lead_ref, c_ref, low, sem = refs[:8], refs[8], refs[9], refs[10], refs[11], refs[12]
    copies = [
        pltpu.make_async_copy(piece.at[64:128], low.at[spot_ref[index]], sem.at[index])
        for index, piece in enumerate(pieces)
    ]
    for copy in copies:
        copy.start()
    for copy in copies:
        copy.wait()
    lead = lead_ref[...]
    for quarter in range(4):
        state = low[:, :, 256 * quarter : 256 * quarter + 256].reshape(512, 256)
        growth = jnp.exp(GROWTH * dot(basis_ref[...], state))
        high, rest = split(growth)
        terms = (dot(lead, high) + dot(lead, rest)) * (1.0 / S)
        c_ref[quarter // 2, :, 256 * (quarter % 2) : 256 * (quarter % 2) + 256] = terms.astype(BF).astype(F32)


def invert(field, inv_ref, out_ref, base, weight):
    lane = lax.broadcasted_iota(jnp.int32, (64, 128), 1)
    first = lane < 64
    for pair in range(8):
        cols = slice(128 * pair, 128 * pair + 128)
        tile = inv_ref[:, cols]
        block = jnp.concatenate([jnp.where(first, tile, 0.0), jnp.where(first, 0.0, tile)], axis=0)
        high, low = split(block)
        fh, fl = split(field[:, cols])
        value = dot(fh, high) + dot(fl, high) + dot(fh, low)
        out_ref[:, cols] = value if base is None else base[:, cols] + weight * value


def pad_modes(value_ref, padded, wp_ref):
    padded[...] = jnp.zeros_like(padded)
    for group in range(4):
        padded[16 * group : 16 * group + 15, :] = value_ref[15 * group : 15 * group + 15, :]
    wp_ref[0:64, :] = padded[...].astype(BF)


def start_body(res_ref, inv_ref, state_ref, w_ref, wp_ref, field, value, padded):
    field[60:64, :] = jnp.zeros((4, NODES), F32)
    field[0:60, :] = state_ref[...]
    wp_ref[64:128, :] = field[...].astype(BF)
    field[60:64, :] = jnp.zeros((4, NODES), F32)
    field[0:60, :] = res_ref[...]
    invert(field, inv_ref, value, None, None)
    w_ref[...] = value[0:60, :]
    pad_modes(value, padded, wp_ref)


def weighted(mine_ref, theirs_ref, grad, cf, half, out_ref, tile):
    for part in range(4):
        left = jnp.concatenate(
            [mine_ref[part].reshape(K * 16, 128), theirs_ref[part].reshape(K * 16, 128)], axis=1
        )
        terms = dot(left, grad)
        total = None
        for k in range(K):
            term = cf[half, k : k + 1, :] * terms[16 * k : 16 * k + 16]
            total = term if total is None else total + term
        out_ref[tile, 16 * part : 16 * part + 16, :] = total.astype(BF)


def along_body(slot_ref, core_ref, *refs):
    blocks = refs[0:8]
    mine_ref, theirs_ref, cf, table_ref, w_ref, trace_ref = refs[8:14]
    f_ref, toward_ref, onward_ref, grads_ref = refs[14:18]
    picked, first_grads, sem = refs[18:21]
    for stored in range(4):
        for index in range(8):

            @pl.when(slot_ref[stored] == index)
            def _(stored=stored, index=index):
                pltpu.make_async_copy(
                    blocks[index].at[0:64], picked.at[stored], sem.at[stored]
                ).start()

    for stored in range(4):
        pltpu.make_async_copy(blocks[0].at[0:64], picked.at[stored], sem.at[stored]).wait()
    core = core_ref[0]
    for pair in range(8):
        tile = picked[:, :, 128 * pair : 128 * pair + 128].reshape(256, 128)
        values = dot(jnp.concatenate([tile, tile], axis=1), table_ref[...]).astype(BF)
        cols = slice(128 * (pair % 4), 128 * (pair % 4) + 128)
        for source in range(16):
            spot = (source // 2) + 8 * (core if source % 2 == 0 else 1 - core)
            for axis in range(3):
                rows = values[16 * source : 16 * source + 16, 128 * axis : 128 * axis + 128]
                if axis == 0:
                    first_grads[pair // 4, spot, :, cols] = rows
                else:
                    grads_ref[2 * (axis - 1) + pair // 4, spot, :, cols] = rows

    def step(half, carry):
        grad = first_grads[half].reshape(256, 512)
        weighted(mine_ref, theirs_ref, grad, cf, half, f_ref, half)
        return carry

    lax.fori_loop(0, 2, step, 0)
    zero = jnp.zeros((4, 512), F32)
    for half in range(2):
        value = (LIFT_SCALE * PENALTY) * jnp.concatenate(
            [w_ref[:, 512 * half : 512 * half + 512], zero], axis=0
        )
        flux = (0.5 * LIFT_SCALE) * f_ref[half].astype(F32)
        for table, mixed, out_ref in (
            (trace_ref[0], value + flux, toward_ref),
            (trace_ref[1], value - flux, onward_ref),
        ):
            high, low = split(mixed)
            out_ref[:, 128 * half : 128 * half + 128] = dot(high, table) + dot(low, table)


def across_body(mine_ref, theirs_ref, cf, grads_ref, f_ref):
    def step(tile, carry):
        grad = grads_ref[tile].reshape(256, 512)
        weighted(mine_ref, theirs_ref, grad, cf, lax.rem(tile, 2), f_ref, tile)
        return carry

    lax.fori_loop(0, 4, step, 0)


def update_body(
    ids_ref, w_ref, fx_ref, f_ref, up_ref, un_ref, res_ref, inv_ref, own_ref, near_ref, count_ref,
    rem_ref, corr_ref, wp_ref, v, faces, rem, value, padded,
):
    lane = lax.broadcasted_iota(jnp.int32, (64, 128), 1)
    first = lane < 64
    v[60:64, :] = jnp.zeros((4, NODES), F32)
    v[0:60, :] = w_ref[...]
    rem[60:64, :] = jnp.zeros((4, NODES), F32)
    rem[0:60, :] = res_ref[...]

    def flux(axis, pair):
        source, index = (fx_ref, pair // 4) if axis == 0 else (f_ref, 2 * (axis - 1) + pair // 4)
        return source[index, :, 128 * (pair % 4) : 128 * (pair % 4) + 128]

    for pair in range(8):
        scaled = (LIFT_SCALE * PENALTY) * v[:, 128 * pair : 128 * pair + 128]
        for axis in (1, 2):
            part = (0.5 * LIFT_SCALE) * flux(axis, pair).astype(F32)
            for side, mixed in enumerate((scaled - part, scaled + part)):
                face = 2 * (axis - 1) + side
                turned = pltpu.roll(mixed, 64, axis=1)
                faces[face, 2 * pair] = jnp.where(first, mixed, turned)
                faces[face, 2 * pair + 1] = jnp.where(first, turned, mixed)
    near = []
    for element in range(16):
        left = jnp.where(first, faces[0, ids_ref[element, 0]], faces[1, ids_ref[element, 1]])
        right = jnp.where(first, faces[2, ids_ref[element, 2]], faces[3, ids_ref[element, 3]])
        high, low = split(jnp.concatenate([left, right], axis=1))
        near.append(dot(high, near_ref[...]) + dot(low, near_ref[...]))
    row = lax.broadcasted_iota(jnp.int32, (256, 128), 0)
    column = lax.broadcasted_iota(jnp.int32, (1, 128), 1)
    inner = column % 64
    uh, ul = split(up_ref[...])
    nh, nl = split(un_ref[...])
    for pair in range(8):
        cols = slice(128 * pair, 128 * pair + 128)
        left, right = 2 * pair, 2 * pair + 1
        below = 16 * jnp.where(column < 64, ids_ref[left, 4], ids_ref[right, 4]) + inner
        above = 16 * jnp.where(column < 64, ids_ref[left, 5], ids_ref[right, 5]) + inner - 48
        lower = jnp.where(row == jnp.where(inner < 16, below, -1), 1.0, 0.0).astype(BF)
        upper = jnp.where(row == jnp.where(inner >= 48, above, -1), 1.0, 0.0).astype(BF)
        across = dot(uh, lower) + dot(ul, lower) + dot(nh, upper) + dot(nl, upper)
        joined = jnp.concatenate([flux(axis, pair) for axis in range(3)], axis=1)
        inside = dot(joined, own_ref[0]) + dot(joined, own_ref[1])
        here = v[:, cols]
        divergence = (
            inside
            + jnp.where(first, near[2 * pair], near[2 * pair + 1])
            + across
            - (LIFT_SCALE * PENALTY) * count_ref[...] * here
        )
        rem[:, cols] = rem[:, cols] - (here - TIME_STEP * divergence)
    invert(rem, inv_ref, value, v, RELAX_WEIGHT)
    rem_ref[...] = rem[0:60, :]
    corr_ref[...] = value[0:60, :]
    pad_modes(value, padded, wp_ref)


def shaped(shape, dtype):
    return jax.ShapeDtypeStruct(shape, dtype)


def pairs_of(count, move):
    return [(index, move(index)) for index in range(count)]


def over_mode(block):
    def along(step):
        return pairs_of(8, lambda i: ((i // 2 + step) % 4) * 2 + i % 2)

    flip = pairs_of(8, lambda i: i ^ 1)
    other = lax.ppermute(block, "mode", flip)
    one = lax.ppermute(block, "mode", along(1))
    two = lax.ppermute(block, "mode", along(2))
    three = lax.ppermute(block, "mode", along(3))
    return [
        block,
        one,
        two,
        three,
        other,
        lax.ppermute(other, "mode", along(1)),
        lax.ppermute(two, "mode", flip),
        lax.ppermute(other, "mode", along(3)),
    ]


def per_device(
    iterate,
    newton_residual,
    inverse_blocks,
    basis_values,
    triple_blocks,
    block_columns,
    neighbour_ids,
):
    mode = lax.axis_index("mode")
    elem = lax.axis_index("elem")
    steps = jnp.arange(8, dtype=jnp.int32)
    spots = ((mode // 2 - steps % 4) % 4) * 2 + ((mode % 2) ^ (steps // 4))
    columns = block_columns[0]
    slots = (mode // 2 - columns // 2) % 4 + 4 * ((mode % 2) ^ (columns % 2))
    core = (elem & 1)[None]
    side = (elem // 8)[None]
    mode_rows = shaped((MB, NODES), F32)
    padded_rows = shaped((ROWS, NODES), BF)
    tile = pltpu.VMEM((ROWS, NODES), F32)

    (stored,) = call(
        stored_body,
        (shaped((PAIRS, 16, 128), BF),),
        (VMEM,),
        (pltpu.VMEM((128, 1280), F32), pltpu.VMEM((1344, 128), F32)),
    )(triple_blocks.reshape(MB, 1260))
    far = lax.ppermute(stored, "elem", pairs_of(16, lambda i: i ^ 8))
    groups = [[8 * zone + 2 * y + c for y in range(4)] for zone in range(2) for c in range(2)]
    sent = jnp.broadcast_to(jnp.stack([stored, far]), (4, 2, PAIRS, 16, 128))
    held = lax.all_to_all(sent, "elem", 0, 0, axis_index_groups=groups)
    correction, padded = call(
        start_body, (mode_rows, shaped((128, NODES), BF)), (VMEM,) * 3, (tile, tile, tile)
    )(newton_residual, inverse_blocks, iterate)
    pieces = over_mode(padded)

    lead = jnp.pad(basis_values[:, :K].T, ((0, 12), (0, 0)))
    spread = jnp.pad(basis_values.reshape(S, 8, MB), ((0, 0), (0, 0), (0, 4))).reshape(S, 512)
    held, spread, lead, slots, spots, ids = lax.optimization_barrier(
        (held, spread, lead, slots, spots, neighbour_ids)
    )
    (mine,) = call(turn_body, (shaped((4, K, 16, 128), BF),), (SMEM,) + (VMEM,) * 2, ())(
        side, held, jnp.asarray(np.eye(128), BF)
    )
    theirs = lax.ppermute(mine, "elem", pairs_of(16, lambda i: i ^ 1))
    (coeffs,) = call(
        coefficient_body,
        (shaped((2, 96, 512), F32),),
        (SMEM,) + (ANY,) * 8 + (VMEM,) * 2,
        (pltpu.VMEM((8, 64, NODES), BF), pltpu.SemaphoreType.DMA((8,))),
    )(spots, *pieces, spread, lead)


    gradients_of = jnp.asarray(gradient_table())
    own = jnp.asarray(own_tables())
    near = jnp.asarray(near_table())
    traces = jnp.asarray(trace_table())
    count = jnp.asarray(face_count())
    remainder = newton_residual
    for sweep in range(ITERS):
        along, toward, onward, grads = call(
            along_body,
            (
                shaped((2, ROWS, 512), BF),
                shaped((ROWS, 256), F32),
                shaped((ROWS, 256), F32),
                shaped((4, 16, 16, 512), BF),
            ),
            (SMEM, SMEM) + (ANY,) * 8 + (VMEM,) * 6,
            (
                pltpu.VMEM((4, ROWS, NODES), BF),
                pltpu.VMEM((2, 16, 16, 512), BF),
                pltpu.SemaphoreType.DMA((4,)),
            ),
        )(slots, core, *pieces, mine, theirs, coeffs, gradients_of, correction, traces)
        after = lax.ppermute(toward, "elem", pairs_of(16, lambda i: (i + 15) % 16))
        before = lax.ppermute(onward, "elem", pairs_of(16, lambda i: (i + 1) % 16))
        (across,) = call(across_body, (shaped((4, ROWS, 512), BF),), (VMEM,) * 4, ())(
            mine, theirs, coeffs, grads
        )
        remainder, correction, padded = call(
            update_body,
            (mode_rows, mode_rows, padded_rows),
            (SMEM,) + (VMEM,) * 10,
            (tile, pltpu.VMEM((4, 16, ROWS, 128), F32), tile, tile, tile),
        )(ids, correction, along, across, before, after, newton_residual, inverse_blocks, own, near, count)
        pieces = over_mode(padded) if sweep + 1 < ITERS else None
    return (correction, remainder)


def solution(mesh):
    return jax.shard_map(
        per_device,
        mesh=mesh,
        in_specs=(
            P("mode", "elem"),
            P("mode", "elem"),
            P(None, "elem"),
            P(),
            P("mode", None, "elem"),
            P("mode", None),
            P("elem", None),
        ),
        out_specs=(P("mode", "elem"), P("mode", "elem")),
        check_vma=False,
    )
```

profile of v0, /device:TPU:0, one launch (start us, length us, event | category | flops | bytes accessed | tf_op | source)
XLA Modules:
  0.0 144.4 jit_solution(1500470368064613084)
XLA Ops:
  0.6 1.9 %shard_map.140 = bf16[42,16,128]{2,1,0:T(8,128)(2,1)} custom-call(bf16[60,1260]{1,0:T(8,128)(2,1)} %bitcast.26), custom_call_target="tpu_custom_call" | custom-call | tf_op jit(solution)/shard_map/pallas_call | solution.py:412
  2.6 4.0 %collective-permute-start = (bf16[42,16,128]{2,1,0:T(8,128)(2,1)}, bf16[42,16,128]{2,1,0:T(8,128)(2,1)S(1)}, u32[]{:S(2)}, u32[]{:S(2)}) collective-permute-start(bf16[42,16,128]{2,1,0:T(8,128)(2,1)} %shard_map.140), channel_id=1, source_target_pairs={{0,64},{8,72},{16,80},{24,88},{32,96},{40,104},{48,112},{56,120},{... | collective-permute-start | bytes 516104 | tf_op jit(solution)/shard_map/ppermute | solution.py:418
  6.5 4.6 %collective-permute-done = bf16[42,16,128]{2,1,0:T(8,128)(2,1)S(1)} collective-permute-done((bf16[42,16,128]{2,1,0:T(8,128)(2,1)}, bf16[42,16,128]{2,1,0:T(8,128)(2,1)S(1)}, u32[]{:S(2)}, u32[]{:S(2)}) %collective-permute-start) | collective-permute-done | bytes 172064 | tf_op jit(solution)/shard_map/ppermute | solution.py:418
  11.1 1.0 pad_maximum_fusion
  12.1 1.3 broadcast_in_dim.9
  13.4 4.6 %all-to-all-start = ((bf16[4,2,42,16,128]{4,3,2,1,0:T(8,128)(2,1)}), bf16[4,2,42,16,128]{4,3,2,1,0:T(8,128)(2,1)S(1)}, u32[]{:S(2)}, u32[]{:S(2)}) async-start(bf16[4,2,42,16,128]{4,3,2,1,0:T(8,128)(2,1)} %broadcast_in_dim.9), calls=%async_computation | async-start | bytes 2752512 | tf_op jit(solution)/shard_map/all_to_all | solution.py:421
  18.3 0.9 slice_bitcast_fusion
  19.2 0.7 pad.9.refs_9_
  20.5 0.6 fusion.slot_ref
  21.1 14.9 %all-to-all-done.held = bf16[4,2,42,16,128]{4,3,2,1,0:T(8,128)(2,1)S(1)} async-done(((bf16[4,2,42,16,128]{4,3,2,1,0:T(8,128)(2,1)}), bf16[4,2,42,16,128]{4,3,2,1,0:T(8,128)(2,1)S(1)}, u32[]{:S(2)}, u32[]{:S(2)}) %all-to-all-start) | async-done | bytes 1376288 | tf_op jit(solution)/shard_map/all_to_all | solution.py:421
  36.0 1.1 copy-done.1
  37.1 4.0 %shard_map.142.refs_8_.mine_ref = bf16[4,84,16,128]{3,2,1,0:T(8,128)(2,1)} custom-call(s32[1]{0:T(128)} %bitcast.7.side_ref, bf16[4,2,42,16,128]{4,3,2,1,0:T(8,128)(2,1)} %copy-done.1, bf16[128,128]{1,0:T(8,128)(2,1)} %constant.119.clone.eye_ref), custom_call_target="tpu_custom_call" | custom-call | tf_op jit(solution)/shard_map/pallas_call | solution.py:432
  41.1 2.3 %shard_map.141 = (f32[60,1024]{1,0:T(8,128)}, bf16[128,1024]{1,0:T(8,128)(2,1)}) custom-call(f32[60,1024]{1,0:T(8,128)} %res_ref.5, f32[64,1024]{1,0:T(8,128)} %inv_ref.5, f32[60,1024]{1,0:T(8,128)} %state_ref.1), custom_call_target="tpu_custom_call" | custom-call | tf_op jit(solution)/shard_map/pallas_call | solution.py:422
  43.3 1.0 collective-permute-start.4
  44.4 3.0 %collective-permute-start.2 = (bf16[128,1024]{1,0:T(8,128)(2,1)}, bf16[128,1024]{1,0:T(8,128)(2,1)S(1)}, u32[]{:S(2)}, u32[]{:S(2)}) collective-permute-start(bf16[128,1024]{1,0:T(8,128)(2,1)} %get-tuple-element.25.refs_0_), channel_id=1, source_target_pairs={{0,4},{1,5},{2,6},{3,7},{4,0},{5,1},{6,2},{7,3},{8,12},{9,13},{10,... | collective-permute-start | bytes 786440 | tf_op jit(solution)/shard_map/ppermute | solution.py:377
  47.4 0.6 collective-permute-start.1
  48.0 2.6 %collective-permute-start.3 = (bf16[128,1024]{1,0:T(8,128)(2,1)}, bf16[128,1024]{1,0:T(8,128)(2,1)S(1)}, u32[]{:S(2)}, u32[]{:S(2)}) collective-permute-start(bf16[128,1024]{1,0:T(8,128)(2,1)} %get-tuple-element.25.refs_0_), channel_id=1, source_target_pairs={{0,6},{1,7},{2,0},{3,1},{4,2},{5,3},{6,4},{7,5},{8,14},{9,15},{10,... | collective-permute-start | bytes 786440 | tf_op jit(solution)/shard_map/ppermute | solution.py:378
  50.6 1.7 %collective-permute-done.4.refs_4_ = bf16[128,1024]{1,0:T(8,128)(2,1)S(1)} collective-permute-done((bf16[128,1024]{1,0:T(8,128)(2,1)}, bf16[128,1024]{1,0:T(8,128)(2,1)S(1)}, u32[]{:S(2)}, u32[]{:S(2)}) %collective-permute-start.4) | collective-permute-done | bytes 262176 | tf_op jit(solution)/shard_map/ppermute | solution.py:375
  52.3 1.5 %collective-permute-start.5 = (bf16[128,1024]{1,0:T(8,128)(2,1)S(1)}, bf16[128,1024]{1,0:T(8,128)(2,1)}, u32[]{:S(2)}, u32[]{:S(2)}) collective-permute-start(bf16[128,1024]{1,0:T(8,128)(2,1)S(1)} %collective-permute-done.4.refs_4_), channel_id=1, source_target_pairs={{0,2},{1,3},{2,4},{3,5},{4,6},{5,7},{6,0},{7,1},{8,10},{9,11},{10,... | collective-permute-start | bytes 786440 | tf_op jit(solution)/shard_map/ppermute | solution.py:385
  53.8 1.5 %collective-permute-done.2.refs_2_ = bf16[128,1024]{1,0:T(8,128)(2,1)S(1)} collective-permute-done((bf16[128,1024]{1,0:T(8,128)(2,1)}, bf16[128,1024]{1,0:T(8,128)(2,1)S(1)}, u32[]{:S(2)}, u32[]{:S(2)}) %collective-permute-start.2) | collective-permute-done | bytes 262176 | tf_op jit(solution)/shard_map/ppermute | solution.py:377
  55.3 2.8 %collective-permute-start.7 = (bf16[128,1024]{1,0:T(8,128)(2,1)S(1)}, bf16[128,1024]{1,0:T(8,128)(2,1)}, u32[]{:S(2)}, u32[]{:S(2)}) collective-permute-start(bf16[128,1024]{1,0:T(8,128)(2,1)S(1)} %collective-permute-done.4.refs_4_), channel_id=1, source_target_pairs={{0,6},{1,7},{2,0},{3,1},{4,2},{5,3},{6,4},{7,5},{8,14},{9,15},{10,... | collective-permute-start | bytes 786440 | tf_op jit(solution)/shard_map/ppermute | solution.py:387
  58.1 2.2 %collective-permute-done.1.refs_1_ = bf16[128,1024]{1,0:T(8,128)(2,1)S(1)} collective-permute-done((bf16[128,1024]{1,0:T(8,128)(2,1)}, bf16[128,1024]{1,0:T(8,128)(2,1)S(1)}, u32[]{:S(2)}, u32[]{:S(2)}) %collective-permute-start.1) | collective-permute-done | bytes 262176 | tf_op jit(solution)/shard_map/ppermute | solution.py:376
  60.2 1.0 collective-permute-start.6
  61.2 1.3 copy.18.refs_8_
  62.6 3.3 %collective-permute-done.5.refs_5_ = bf16[128,1024]{1,0:T(8,128)(2,1)} collective-permute-done((bf16[128,1024]{1,0:T(8,128)(2,1)S(1)}, bf16[128,1024]{1,0:T(8,128)(2,1)}, u32[]{:S(2)}, u32[]{:S(2)}) %collective-permute-start.5) | collective-permute-done | bytes 262176 | tf_op jit(solution)/shard_map/ppermute | solution.py:385
  66.0 2.5 %collective-permute-done.6.refs_6_ = bf16[128,1024]{1,0:T(8,128)(2,1)} collective-permute-done((bf16[128,1024]{1,0:T(8,128)(2,1)S(1)}, bf16[128,1024]{1,0:T(8,128)(2,1)}, u32[]{:S(2)}, u32[]{:S(2)}) %collective-permute-start.6) | collective-permute-done | bytes 262176 | tf_op jit(solution)/shard_map/ppermute | solution.py:386
  68.5 6.9 %shard_map.143.refs_10_.cf = f32[2,96,512]{2,1,0:T(8,128)} custom-call(s32[8]{0:T(128)} %fusion.5.spot_ref, bf16[128,1024]{1,0:T(8,128)(2,1)} %get-tuple-element.25.refs_0_, bf16[128,1024]{1,0:T(8,128)(2,1)} %copy-done.5, bf16[128,1024]{1,0:T(8,128)(2,1)} %copy-done.4, bf16[128,1024]{1,0:T(8,128)(2,1)} %copy-done.6, bf16[128,1024]{1,0:T(8,128)(2,1)} %copy-done.3, ...), custom_call_target="tpu_custom_call" | custom-call | tf_op jit(solution)/shard_map/pallas_call | solution.py:436
  75.4 1.1 copy-done
  76.5 8.0 %shard_map.144 = (bf16[2,64,512]{2,1,0:T(8,128)(2,1)}, f32[64,256]{1,0:T(8,128)}, f32[64,256]{1,0:T(8,128)}, bf16[4,16,16,512]{3,2,1,0:T(8,128)(2,1)}) custom-call(s32[4]{0:T(128)} %fusion.slot_ref, s32[1]{0:T(128)} %bitcast.6.core_ref, bf16[128,1024]{1,0:T(8,128)(2,1)} %get-tuple-element.25.refs_0_, bf16[128,1024]{1,0:T(8,128)(2,1)} %copy-done.5, ...), custom_call_target="tpu_custom_call" | custom-call | tf_op jit(solution)/shard_map/pallas_call | solution.py:451
  84.5 2.9 %collective-permute-start.10 = (f32[64,256]{1,0:T(8,128)}, f32[64,256]{1,0:T(8,128)S(1)}, u32[]{:S(2)}, u32[]{:S(2)}) collective-permute-start(f32[64,256]{1,0:T(8,128)} %get-tuple-element.33), channel_id=1, source_target_pairs={{0,120},{8,0},{16,8},{24,16},{32,24},{40,32},{48,40},{56,48},{64,5... | collective-permute-start | bytes 196616 | tf_op jit(solution)/shard_map/ppermute | solution.py:466
  87.4 0.7 copy.20.ids_ref
  88.1 9.3 %shard_map.145.f_ref = bf16[4,64,512]{2,1,0:T(8,128)(2,1)} custom-call(bf16[4,84,16,128]{3,2,1,0:T(8,128)(2,1)} %shard_map.142.refs_8_.mine_ref, bf16[4,84,16,128]{3,2,1,0:T(8,128)(2,1)} %copy-done, f32[2,96,512]{2,1,0:T(8,128)} %shard_map.143.refs_10_.cf, bf16[4,16,16,512]{3,2,1,0:T(8,128)(2,1)} %get-tuple-element.31.grads_ref), custom_call_target="tpu_custom_call" | custom-call | tf_op jit(solution)/shard_map/pallas_call | solution.py:468
  97.4 0.6 copy-done.16
  98.1 3.7 %shard_map.146 = (f32[60,1024]{1,0:T(8,128)}, f32[60,1024]{1,0:T(8,128)}, bf16[64,1024]{1,0:T(8,128)(2,1)}) custom-call(s32[16,6]{1,0:T(8,128)} %copy.20.ids_ref, f32[60,1024]{1,0:T(8,128)} %get-tuple-element.23.refs_12_.w_ref, bf16[2,64,512]{2,1,0:T(8,128)(2,1)} %get-tuple-element.30.fx_ref, bf16[4,64,512]{2,1,0:T(8,128)(2,1)} %shard_map.145.f_ref, ...), custom_call_target="tpu_custom_call" | custom-call | tf_op jit(solution)/shard_map/pallas_call | solution.py:471
  102.0 1.7 %collective-permute-start.11 = (bf16[64,1024]{1,0:T(8,128)(2,1)}, bf16[64,1024]{1,0:T(8,128)(2,1)S(1)}, u32[]{:S(2)}, u32[]{:S(2)}) collective-permute-start(bf16[64,1024]{1,0:T(8,128)(2,1)} %get-tuple-element.35.refs_0_), channel_id=1, source_target_pairs={{0,2},{1,3},{2,4},{3,5},{4,6},{5,7},{6,0},{7,1},{8,10},{9,11},{10,... | collective-permute-start | bytes 393224 | tf_op jit(solution)/shard_map/ppermute | solution.py:376
  103.8 1.5 %collective-permute-start.13 = (bf16[64,1024]{1,0:T(8,128)(2,1)}, bf16[64,1024]{1,0:T(8,128)(2,1)S(1)}, u32[]{:S(2)}, u32[]{:S(2)}) collective-permute-start(bf16[64,1024]{1,0:T(8,128)(2,1)} %get-tuple-element.35.refs_0_), channel_id=1, source_target_pairs={{0,6},{1,7},{2,0},{3,1},{4,2},{5,3},{6,4},{7,5},{8,14},{9,15},{10,... | collective-permute-start | bytes 393224 | tf_op jit(solution)/shard_map/ppermute | solution.py:378
  105.3 1.7 %collective-permute-done.14.refs_4_ = bf16[64,1024]{1,0:T(8,128)(2,1)S(1)} collective-permute-done((bf16[64,1024]{1,0:T(8,128)(2,1)}, bf16[64,1024]{1,0:T(8,128)(2,1)S(1)}, u32[]{:S(2)}, u32[]{:S(2)}) %collective-permute-start.14) | collective-permute-done | bytes 131104 | tf_op jit(solution)/shard_map/ppermute | solution.py:375
  107.0 2.9 %collective-permute-done.12.refs_2_ = bf16[64,1024]{1,0:T(8,128)(2,1)S(1)} collective-permute-done((bf16[64,1024]{1,0:T(8,128)(2,1)}, bf16[64,1024]{1,0:T(8,128)(2,1)S(1)}, u32[]{:S(2)}, u32[]{:S(2)}) %collective-permute-start.12) | collective-permute-done | bytes 131104 | tf_op jit(solution)/shard_map/ppermute | solution.py:377
  109.9 1.8 %collective-permute-start.16 = (bf16[64,1024]{1,0:T(8,128)(2,1)S(1)}, bf16[64,1024]{1,0:T(8,128)(2,1)S(1)}, u32[]{:S(2)}, u32[]{:S(2)}) collective-permute-start(bf16[64,1024]{1,0:T(8,128)(2,1)S(1)} %collective-permute-done.12.refs_2_), channel_id=1, source_target_pairs={{0,1},{1,0},{2,3},{3,2},{4,5},{5,4},{6,7},{7,6},{8,9},{9,8},{10,11... | collective-permute-start | bytes 393224 | tf_op jit(solution)/shard_map/ppermute | solution.py:386
  111.7 1.6 %collective-permute-done.15.refs_5_ = bf16[64,1024]{1,0:T(8,128)(2,1)S(1)} collective-permute-done((bf16[64,1024]{1,0:T(8,128)(2,1)S(1)}, bf16[64,1024]{1,0:T(8,128)(2,1)S(1)}, u32[]{:S(2)}, u32[]{:S(2)}) %collective-permute-start.15) | collective-permute-done | bytes 131104 | tf_op jit(solution)/shard_map/ppermute | solution.py:385
  113.3 1.5 %collective-permute-done.16.refs_6_ = bf16[64,1024]{1,0:T(8,128)(2,1)S(1)} collective-permute-done((bf16[64,1024]{1,0:T(8,128)(2,1)S(1)}, bf16[64,1024]{1,0:T(8,128)(2,1)S(1)}, u32[]{:S(2)}, u32[]{:S(2)}) %collective-permute-start.16) | collective-permute-done | bytes 131104 | tf_op jit(solution)/shard_map/ppermute | solution.py:386
  114.9 1.8 %collective-permute-done.17.refs_7_ = bf16[64,1024]{1,0:T(8,128)(2,1)S(1)} collective-permute-done((bf16[64,1024]{1,0:T(8,128)(2,1)S(1)}, bf16[64,1024]{1,0:T(8,128)(2,1)S(1)}, u32[]{:S(2)}, u32[]{:S(2)}) %collective-permute-start.17) | collective-permute-done | bytes 131104 | tf_op jit(solution)/shard_map/ppermute | solution.py:387
  116.7 0.6 copy-done.13
  117.3 8.0 %shard_map.147 = (bf16[2,64,512]{2,1,0:T(8,128)(2,1)}, f32[64,256]{1,0:T(8,128)}, f32[64,256]{1,0:T(8,128)}, bf16[4,16,16,512]{3,2,1,0:T(8,128)(2,1)}) custom-call(s32[4]{0:T(128)} %fusion.slot_ref, s32[1]{0:T(128)} %bitcast.6.core_ref, bf16[64,1024]{1,0:T(8,128)(2,1)} %get-tuple-element.35.refs_0_, bf16[64,1024]{1,0:T(8,128)(2,1)} %copy-done.9, ...), custom_call_target="tpu_custom_call" | custom-call | tf_op jit(solution)/shard_map/pallas_call | solution.py:451
  125.4 5.3 %collective-permute-start.19 = (f32[64,256]{1,0:T(8,128)}, f32[64,256]{1,0:T(8,128)S(1)}, u32[]{:S(2)}, u32[]{:S(2)}) collective-permute-start(f32[64,256]{1,0:T(8,128)} %get-tuple-element.39), channel_id=1, source_target_pairs={{0,120},{8,0},{16,8},{24,16},{32,24},{40,32},{48,40},{56,48},{64,5... | collective-permute-start | bytes 196616 | tf_op jit(solution)/shard_map/ppermute | solution.py:466
  130.8 9.3 %shard_map.148.f_ref = bf16[4,64,512]{2,1,0:T(8,128)(2,1)} custom-call(bf16[4,84,16,128]{3,2,1,0:T(8,128)(2,1)} %shard_map.142.refs_8_.mine_ref, bf16[4,84,16,128]{3,2,1,0:T(8,128)(2,1)} %copy-done, f32[2,96,512]{2,1,0:T(8,128)} %shard_map.143.refs_10_.cf, bf16[4,16,16,512]{3,2,1,0:T(8,128)(2,1)} %get-tuple-element.37.grads_ref), custom_call_target="tpu_custom_call" | custom-call | tf_op jit(solution)/shard_map/pallas_call | solution.py:468
  140.1 0.6 copy-done.14
  140.7 3.7 %shard_map.149 = (f32[60,1024]{1,0:T(8,128)}, f32[60,1024]{1,0:T(8,128)}, bf16[64,1024]{1,0:T(8,128)(2,1)}) custom-call(s32[16,6]{1,0:T(8,128)} %copy.20.ids_ref, f32[60,1024]{1,0:T(8,128)} %get-tuple-element.34.refs_12_.w_ref, bf16[2,64,512]{2,1,0:T(8,128)(2,1)} %get-tuple-element.36.fx_ref, bf16[4,64,512]{2,1,0:T(8,128)(2,1)} %shard_map.148.f_ref, ...), custom_call_target="tpu_custom_call" | custom-call | tf_op jit(solution)/shard_map/pallas_call | solution.py:471
  (54 shorter events, 1.5 us)
Async XLA Ops:
  2.6 8.6 %collective-permute-start = (bf16[42,16,128]{2,1,0:T(8,128)(2,1)}, bf16[42,16,128]{2,1,0:T(8,128)(2,1)S(1)}, u32[]{:S(2)}, u32[]{:S(2)}) collective-permute-start(bf16[42,16,128]{2,1,0:T(8,128)(2,1)} %shard_map.140), channel_id=1, source_target_pairs={{0,64},{8,72},{16,80},{24,88},{32,96},{40,104},{48,112},{56,120},{... | collective-permute-start | bytes 516104 | tf_op jit(solution)/shard_map/ppermute | solution.py:418
  13.4 4.6 %copy-start.2 = (bf16[1024,480]{0,1:T(8,128)(2,1)S(1)}, bf16[1024,480]{0,1:T(8,128)(2,1)}, u32[]{:S(2)}) copy-start(bf16[1024,480]{0,1:T(8,128)(2,1)} %param.16) | copy-start | bytes 2949124
  13.4 22.6 %all-to-all-start = ((bf16[4,2,42,16,128]{4,3,2,1,0:T(8,128)(2,1)}), bf16[4,2,42,16,128]{4,3,2,1,0:T(8,128)(2,1)S(1)}, u32[]{:S(2)}, u32[]{:S(2)}) async-start(bf16[4,2,42,16,128]{4,3,2,1,0:T(8,128)(2,1)} %broadcast_in_dim.9), calls=%async_computation | async-start | bytes 2752512 | tf_op jit(solution)/shard_map/all_to_all | solution.py:421
  18.2 2.3 %copy-start.19 = (s32[1,4]{1,0:T(1,128)S(1)}, s32[1,4]{1,0:T(1,128)}, u32[]{:S(2)}) copy-start(s32[1,4]{1,0:T(1,128)} %param.18) | copy-start | bytes 52
  36.0 1.1 copy-start.1
  41.1 34.3 %collective-permute-start.8 = (bf16[4,84,16,128]{3,2,1,0:T(8,128)(2,1)}, bf16[4,84,16,128]{3,2,1,0:T(8,128)(2,1)S(1)}, u32[]{:S(2)}, u32[]{:S(2)}) collective-permute-start(bf16[4,84,16,128]{3,2,1,0:T(8,128)(2,1)} %shard_map.142.refs_8_.mine_ref), channel_id=1, source_target_pairs={{0,8},{8,0},{16,24},{24,16},{32,40},{40,32},{48,56},{56,48},{64,72... | collective-permute-start | bytes 4128776 | tf_op jit(solution)/shard_map/ppermute | solution.py:435
  43.3 8.9 %collective-permute-start.4 = (bf16[128,1024]{1,0:T(8,128)(2,1)}, bf16[128,1024]{1,0:T(8,128)(2,1)S(1)}, u32[]{:S(2)}, u32[]{:S(2)}) collective-permute-start(bf16[128,1024]{1,0:T(8,128)(2,1)} %get-tuple-element.25.refs_0_), channel_id=1, source_target_pairs={{0,1},{1,0},{2,3},{3,2},{4,5},{5,4},{6,7},{7,6},{8,9},{9,8},{10,11... | collective-permute-start | bytes 786440 | tf_op jit(solution)/shard_map/ppermute | solution.py:375
  44.4 10.9 %collective-permute-start.2 = (bf16[128,1024]{1,0:T(8,128)(2,1)}, bf16[128,1024]{1,0:T(8,128)(2,1)S(1)}, u32[]{:S(2)}, u32[]{:S(2)}) collective-permute-start(bf16[128,1024]{1,0:T(8,128)(2,1)} %get-tuple-element.25.refs_0_), channel_id=1, source_target_pairs={{0,4},{1,5},{2,6},{3,7},{4,0},{5,1},{6,2},{7,3},{8,12},{9,13},{10,... | collective-permute-start | bytes 786440 | tf_op jit(solution)/shard_map/ppermute | solution.py:377
  47.4 12.8 %collective-permute-start.1 = (bf16[128,1024]{1,0:T(8,128)(2,1)}, bf16[128,1024]{1,0:T(8,128)(2,1)S(1)}, u32[]{:S(2)}, u32[]{:S(2)}) collective-permute-start(bf16[128,1024]{1,0:T(8,128)(2,1)} %get-tuple-element.25.refs_0_), channel_id=1, source_target_pairs={{0,2},{1,3},{2,4},{3,5},{4,6},{5,7},{6,0},{7,1},{8,10},{9,11},{10,... | collective-permute-start | bytes 786440 | tf_op jit(solution)/shard_map/ppermute | solution.py:376
  48.0 14.6 %collective-permute-start.3 = (bf16[128,1024]{1,0:T(8,128)(2,1)}, bf16[128,1024]{1,0:T(8,128)(2,1)S(1)}, u32[]{:S(2)}, u32[]{:S(2)}) collective-permute-start(bf16[128,1024]{1,0:T(8,128)(2,1)} %get-tuple-element.25.refs_0_), channel_id=1, source_target_pairs={{0,6},{1,7},{2,0},{3,1},{4,2},{5,3},{6,4},{7,5},{8,14},{9,15},{10,... | collective-permute-start | bytes 786440 | tf_op jit(solution)/shard_map/ppermute | solution.py:378
  52.3 16.2 %copy-start.3 = (bf16[128,1024]{1,0:T(8,128)(2,1)}, bf16[128,1024]{1,0:T(8,128)(2,1)S(1)}, u32[]{:S(2)}) copy-start(bf16[128,1024]{1,0:T(8,128)(2,1)S(1)} %collective-permute-done.4.refs_4_) | copy-start | bytes 786436
  52.3 13.6 %collective-permute-start.5 = (bf16[128,1024]{1,0:T(8,128)(2,1)S(1)}, bf16[128,1024]{1,0:T(8,128)(2,1)}, u32[]{:S(2)}, u32[]{:S(2)}) collective-permute-start(bf16[128,1024]{1,0:T(8,128)(2,1)S(1)} %collective-permute-done.4.refs_4_), channel_id=1, source_target_pairs={{0,2},{1,3},{2,4},{3,5},{4,6},{5,7},{6,0},{7,1},{8,10},{9,11},{10,... | collective-permute-start | bytes 786440 | tf_op jit(solution)/shard_map/ppermute | solution.py:385
  55.3 13.2 %copy-start.4 = (bf16[128,1024]{1,0:T(8,128)(2,1)}, bf16[128,1024]{1,0:T(8,128)(2,1)S(1)}, u32[]{:S(2)}) copy-start(bf16[128,1024]{1,0:T(8,128)(2,1)S(1)} %collective-permute-done.2.refs_2_) | copy-start | bytes 786436
  55.3 10.7 %collective-permute-start.7 = (bf16[128,1024]{1,0:T(8,128)(2,1)S(1)}, bf16[128,1024]{1,0:T(8,128)(2,1)}, u32[]{:S(2)}, u32[]{:S(2)}) collective-permute-start(bf16[128,1024]{1,0:T(8,128)(2,1)S(1)} %collective-permute-done.4.refs_4_), channel_id=1, source_target_pairs={{0,6},{1,7},{2,0},{3,1},{4,2},{5,3},{6,4},{7,5},{8,14},{9,15},{10,... | collective-permute-start | bytes 786440 | tf_op jit(solution)/shard_map/ppermute | solution.py:387
  60.2 8.2 %copy-start.5 = (bf16[128,1024]{1,0:T(8,128)(2,1)}, bf16[128,1024]{1,0:T(8,128)(2,1)S(1)}, u32[]{:S(2)}) copy-start(bf16[128,1024]{1,0:T(8,128)(2,1)S(1)} %collective-permute-done.1.refs_1_) | copy-start | bytes 786436
  60.2 8.2 %collective-permute-start.6 = (bf16[128,1024]{1,0:T(8,128)(2,1)S(1)}, bf16[128,1024]{1,0:T(8,128)(2,1)}, u32[]{:S(2)}, u32[]{:S(2)}) collective-permute-start(bf16[128,1024]{1,0:T(8,128)(2,1)S(1)} %collective-permute-done.2.refs_2_), channel_id=1, source_target_pairs={{0,1},{1,0},{2,3},{3,2},{4,5},{5,4},{6,7},{7,6},{8,9},{9,8},{10,11... | collective-permute-start | bytes 786440 | tf_op jit(solution)/shard_map/ppermute | solution.py:386
  62.6 5.9 %copy-start.6 = (bf16[128,1024]{1,0:T(8,128)(2,1)}, bf16[128,1024]{1,0:T(8,128)(2,1)S(1)}, u32[]{:S(2)}) copy-start(bf16[128,1024]{1,0:T(8,128)(2,1)S(1)} %collective-permute-done.3.refs_3_) | copy-start | bytes 786436
  75.4 1.1 copy-start
  76.5 11.0 %copy-start.18 = (s32[16,6]{0,1:T(8,128)S(1)}, s32[16,6]{0,1:T(8,128)}, u32[]{:S(2)}) copy-start(s32[16,6]{0,1:T(8,128)} %param.19) | copy-start | bytes 1156
  84.5 12.9 %collective-permute-start.10 = (f32[64,256]{1,0:T(8,128)}, f32[64,256]{1,0:T(8,128)S(1)}, u32[]{:S(2)}, u32[]{:S(2)}) collective-permute-start(f32[64,256]{1,0:T(8,128)} %get-tuple-element.33), channel_id=1, source_target_pairs={{0,120},{8,0},{16,8},{24,16},{32,24},{40,32},{48,40},{56,48},{64,5... | collective-permute-start | bytes 196616 | tf_op jit(solution)/shard_map/ppermute | solution.py:466
  87.4 10.0 %collective-permute-start.9 = (f32[64,256]{1,0:T(8,128)}, f32[64,256]{1,0:T(8,128)S(1)}, u32[]{:S(2)}, u32[]{:S(2)}) collective-permute-start(f32[64,256]{1,0:T(8,128)} %get-tuple-element.32), channel_id=1, source_target_pairs={{0,8},{8,16},{16,24},{24,32},{32,40},{40,48},{48,56},{56,64},{64,7... | collective-permute-start | bytes 196616 | tf_op jit(solution)/shard_map/ppermute | solution.py:467
  97.4 0.6 copy-start.16
  97.4 0.6 copy-start.17
  101.8 5.2 %collective-permute-start.14 = (bf16[64,1024]{1,0:T(8,128)(2,1)}, bf16[64,1024]{1,0:T(8,128)(2,1)S(1)}, u32[]{:S(2)}, u32[]{:S(2)}) collective-permute-start(bf16[64,1024]{1,0:T(8,128)(2,1)} %get-tuple-element.35.refs_0_), channel_id=1, source_target_pairs={{0,1},{1,0},{2,3},{3,2},{4,5},{5,4},{6,7},{7,6},{8,9},{9,8},{10,11... | collective-permute-start | bytes 393224 | tf_op jit(solution)/shard_map/ppermute | solution.py:375
  101.8 8.1 %collective-permute-start.12 = (bf16[64,1024]{1,0:T(8,128)(2,1)}, bf16[64,1024]{1,0:T(8,128)(2,1)S(1)}, u32[]{:S(2)}, u32[]{:S(2)}) collective-permute-start(bf16[64,1024]{1,0:T(8,128)(2,1)} %get-tuple-element.35.refs_0_), channel_id=1, source_target_pairs={{0,4},{1,5},{2,6},{3,7},{4,0},{5,1},{6,2},{7,3},{8,12},{9,13},{10,... | collective-permute-start | bytes 393224 | tf_op jit(solution)/shard_map/ppermute | solution.py:377
  102.0 9.7 %collective-permute-start.11 = (bf16[64,1024]{1,0:T(8,128)(2,1)}, bf16[64,1024]{1,0:T(8,128)(2,1)S(1)}, u32[]{:S(2)}, u32[]{:S(2)}) collective-permute-start(bf16[64,1024]{1,0:T(8,128)(2,1)} %get-tuple-element.35.refs_0_), channel_id=1, source_target_pairs={{0,2},{1,3},{2,4},{3,5},{4,6},{5,7},{6,0},{7,1},{8,10},{9,11},{10,... | collective-permute-start | bytes 393224 | tf_op jit(solution)/shard_map/ppermute | solution.py:376
  103.8 8.0 %collective-permute-start.13 = (bf16[64,1024]{1,0:T(8,128)(2,1)}, bf16[64,1024]{1,0:T(8,128)(2,1)S(1)}, u32[]{:S(2)}, u32[]{:S(2)}) collective-permute-start(bf16[64,1024]{1,0:T(8,128)(2,1)} %get-tuple-element.35.refs_0_), channel_id=1, source_target_pairs={{0,6},{1,7},{2,0},{3,1},{4,2},{5,3},{6,4},{7,5},{8,14},{9,15},{10,... | collective-permute-start | bytes 393224 | tf_op jit(solution)/shard_map/ppermute | solution.py:378
  107.0 9.7 %copy-start.7 = (bf16[64,1024]{1,0:T(8,128)(2,1)}, bf16[64,1024]{1,0:T(8,128)(2,1)S(1)}, u32[]{:S(2)}) copy-start(bf16[64,1024]{1,0:T(8,128)(2,1)S(1)} %collective-permute-done.14.refs_4_) | copy-start | bytes 393220
  107.0 6.4 %collective-permute-start.15 = (bf16[64,1024]{1,0:T(8,128)(2,1)S(1)}, bf16[64,1024]{1,0:T(8,128)(2,1)S(1)}, u32[]{:S(2)}, u32[]{:S(2)}) collective-permute-start(bf16[64,1024]{1,0:T(8,128)(2,1)S(1)} %collective-permute-done.14.refs_4_), channel_id=1, source_target_pairs={{0,2},{1,3},{2,4},{3,5},{4,6},{5,7},{6,0},{7,1},{8,10},{9,11},{10,... | collective-permute-start | bytes 393224 | tf_op jit(solution)/shard_map/ppermute | solution.py:385
  109.9 6.7 %copy-start.8 = (bf16[64,1024]{1,0:T(8,128)(2,1)}, bf16[64,1024]{1,0:T(8,128)(2,1)S(1)}, u32[]{:S(2)}) copy-start(bf16[64,1024]{1,0:T(8,128)(2,1)S(1)} %collective-permute-done.12.refs_2_) | copy-start | bytes 393220
  109.9 5.0 %collective-permute-start.16 = (bf16[64,1024]{1,0:T(8,128)(2,1)S(1)}, bf16[64,1024]{1,0:T(8,128)(2,1)S(1)}, u32[]{:S(2)}, u32[]{:S(2)}) collective-permute-start(bf16[64,1024]{1,0:T(8,128)(2,1)S(1)} %collective-permute-done.12.refs_2_), channel_id=1, source_target_pairs={{0,1},{1,0},{2,3},{3,2},{4,5},{5,4},{6,7},{7,6},{8,9},{9,8},{10,11... | collective-permute-start | bytes 393224 | tf_op jit(solution)/shard_map/ppermute | solution.py:386
  111.7 5.0 %collective-permute-start.17 = (bf16[64,1024]{1,0:T(8,128)(2,1)S(1)}, bf16[64,1024]{1,0:T(8,128)(2,1)S(1)}, u32[]{:S(2)}, u32[]{:S(2)}) collective-permute-start(bf16[64,1024]{1,0:T(8,128)(2,1)S(1)} %collective-permute-done.14.refs_4_), channel_id=1, source_target_pairs={{0,6},{1,7},{2,0},{3,1},{4,2},{5,3},{6,4},{7,5},{8,14},{9,15},{10,... | collective-permute-start | bytes 393224 | tf_op jit(solution)/shard_map/ppermute | solution.py:387
  111.7 4.9 %copy-start.9 = (bf16[64,1024]{1,0:T(8,128)(2,1)}, bf16[64,1024]{1,0:T(8,128)(2,1)S(1)}, u32[]{:S(2)}) copy-start(bf16[64,1024]{1,0:T(8,128)(2,1)S(1)} %collective-permute-done.11.refs_1_) | copy-start | bytes 393220
  111.7 4.9 %copy-start.10 = (bf16[64,1024]{1,0:T(8,128)(2,1)}, bf16[64,1024]{1,0:T(8,128)(2,1)S(1)}, u32[]{:S(2)}) copy-start(bf16[64,1024]{1,0:T(8,128)(2,1)S(1)} %collective-permute-done.13.refs_3_) | copy-start | bytes 393220
  113.3 3.3 %copy-start.11 = (bf16[64,1024]{1,0:T(8,128)(2,1)}, bf16[64,1024]{1,0:T(8,128)(2,1)S(1)}, u32[]{:S(2)}) copy-start(bf16[64,1024]{1,0:T(8,128)(2,1)S(1)} %collective-permute-done.15.refs_5_) | copy-start | bytes 393220
  114.9 1.8 %copy-start.12 = (bf16[64,1024]{1,0:T(8,128)(2,1)}, bf16[64,1024]{1,0:T(8,128)(2,1)S(1)}, u32[]{:S(2)}) copy-start(bf16[64,1024]{1,0:T(8,128)(2,1)S(1)} %collective-permute-done.16.refs_6_) | copy-start | bytes 393220
  116.6 0.7 copy-start.13
  125.3 14.7 %collective-permute-start.18 = (f32[64,256]{1,0:T(8,128)}, f32[64,256]{1,0:T(8,128)S(1)}, u32[]{:S(2)}, u32[]{:S(2)}) collective-permute-start(f32[64,256]{1,0:T(8,128)} %get-tuple-element.38), channel_id=1, source_target_pairs={{0,8},{8,16},{16,24},{24,32},{32,40},{40,48},{48,56},{56,64},{64,7... | collective-permute-start | bytes 196616 | tf_op jit(solution)/shard_map/ppermute | solution.py:467
  125.4 14.6 %collective-permute-start.19 = (f32[64,256]{1,0:T(8,128)}, f32[64,256]{1,0:T(8,128)S(1)}, u32[]{:S(2)}, u32[]{:S(2)}) collective-permute-start(f32[64,256]{1,0:T(8,128)} %get-tuple-element.39), channel_id=1, source_target_pairs={{0,120},{8,0},{16,8},{24,16},{32,24},{40,32},{48,40},{56,48},{64,5... | collective-permute-start | bytes 196616 | tf_op jit(solution)/shard_map/ppermute | solution.py:466
  140.0 0.6 copy-start.14
  140.1 0.7 copy-start.15
where the time goes:
time: 145 us; the launch traced here: 144 us
  Pallas kernels  57.2 us (39%)
  waiting for transfers between devices  40.3 us (28%)
  starting transfers between devices  34.8 us (24%)
  local copies, waits for them, and re-layouts  9.31 us (6%)
  other arithmetic  2.09 us (1%)
    pallas_call x2, Pallas kernels, per_device(): call(across_body, (shaped((4, ROWS, 512), BF),), (VMEM,) * 4, ())  18.6 us
    pallas_call x2, Pallas kernels, per_device(): call(along_body, (shaped((2, ROWS, 512), BF), shaped((ROWS, 256), F32), s...  16.1 us
    all_to_all x1, waiting for transfers between devices, per_device(): held = lax.all_to_all(sent, 'elem', 0, 0, axis_index_groups=groups)  14.9 us
    ppermute x2, starting transfers between devices, per_device(): after = lax.ppermute(toward, 'elem', pairs_of(16, lambda i: (i + 15) % 16))  8.27 us
    pallas_call x2, Pallas kernels, per_device(): call(update_body, (mode_rows, mode_rows, padded_rows), (SMEM,) + (VMEM,)...  7.45 us
    pallas_call x1, Pallas kernels, per_device(): call(coefficient_body, (shaped((2, 96, 512), F32),), (SMEM,) + (ANY,) * 8...  6.9 us
    ppermute x2, waiting for transfers between devices, over_mode(): lax.ppermute(other, 'mode', along(1))  4.89 us
    all_to_all x1, starting transfers between devices, per_device(): held = lax.all_to_all(sent, 'elem', 0, 0, axis_index_groups=groups)  4.59 us
  transfers between devices with their start and end apart: 21, of which 13 were waited for; matrix products, arithmetic and copies ran while one was open for 3% of the time, Pallas kernels for 19%

commit v1 on v0

--- a/solution.py
+++ b/solution.py
@@ -26,6 +26,7 @@
 VMEM = pl.BlockSpec(memory_space=pltpu.VMEM)
 SMEM = pl.BlockSpec(memory_space=pltpu.SMEM)
 ANY = pl.BlockSpec(memory_space=pl.ANY)
+FAR = pl.BlockSpec(memory_space=pltpu.HBM)
 
 
 def line_derivative():
@@ -130,7 +131,7 @@
     return high, (value - high.astype(F32)).astype(BF)
 
 
-def call(body, outs, ins, scratch=(), limit=56 << 20):
+def call(body, outs, ins, scratch=(), limit=20 << 20):
     specs = [VMEM if isinstance(o, jax.ShapeDtypeStruct) else o for o in outs]
     return pl.pallas_call(
         body,
@@ -140,6 +141,16 @@
         scratch_shapes=list(scratch),
         compiler_params=pltpu.CompilerParams(vmem_limit_bytes=limit),
     )
+
+
+def fetch(sources, targets, sem):
+    copies = [
+        pltpu.make_async_copy(source, target, sem.at[index])
+        for index, (source, target) in enumerate(zip(sources, targets))
+    ]
+    for copy in copies:
+        copy.start()
+    return copies
 
 
 def stored_body(x_ref, z_ref, wide, tall):
@@ -154,7 +165,7 @@
         z_ref[pair] = tall[pl.ds(2 * pair, 16, stride=K), :].astype(BF)
 
 
-def turn_body(side_ref, held, eye_ref, tt_ref):
+def turn_body(side_ref, ids_ref, held, eye_ref, tt_ref):
     side = side_ref[0]
 
     def step(twin, carry):
@@ -179,19 +190,25 @@
 
 
 def coefficient_body(spot_ref, *refs):
-    pieces, basis_ref, lead_ref, c_ref, low, sem = refs[:8], refs[8], refs[9], refs[10], refs[11], refs[12]
-    copies = [
-        pltpu.make_async_copy(piece.at[64:128], low.at[spot_ref[index]], sem.at[index])
-        for index, piece in enumerate(pieces)
-    ]
-    for copy in copies:
-        copy.start()
-    for copy in copies:
+    pieces, turned_ref, c_ref = refs[:8], refs[8], refs[9]
+    low, joined, turned, basis, sem = refs[10:15]
+    copies = fetch(
+        [piece.at[64:128] for piece in pieces] + [turned_ref],
+        [low.at[spot_ref[index]] for index in range(8)] + [turned],
+        sem,
+    )
+    copies[8].wait()
+    for block in range(8):
+        rows = turned[:, 128 * block : 128 * block + 128].astype(F32).T
+        basis[128 * block : 128 * block + 128, :] = rows.astype(BF)
+    lead = turned[0:96, :]
+    for copy in copies[:8]:
         copy.wait()
-    lead = lead_ref[...]
+    for block in range(8):
+        joined[60 * block : 60 * block + 60, :] = low[block].astype(F32)[0:60]
     for quarter in range(4):
-        state = low[:, :, 256 * quarter : 256 * quarter + 256].reshape(512, 256)
-        growth = jnp.exp(GROWTH * dot(basis_ref[...], state))
+        state = joined[:, 256 * quarter : 256 * quarter + 256].astype(BF)
+        growth = jnp.exp(GROWTH * dot(basis[...], state))
         high, rest = split(growth)
         terms = (dot(lead, high) + dot(lead, rest)) * (1.0 / S)
         c_ref[quarter // 2, :, 256 * (quarter % 2) : 256 * (quarter % 2) + 256] = terms.astype(BF).astype(F32)
@@ -217,13 +234,18 @@
     wp_ref[0:64, :] = padded[...].astype(BF)
 
 
-def start_body(res_ref, inv_ref, state_ref, w_ref, wp_ref, field, value, padded):
+def start_body(
+    res_ref, inv_ref, state_ref, w_ref, wp_ref, field, value, padded, res, inverse, state, sem
+):
+    copies = fetch((state_ref, res_ref, inv_ref), (state, res, inverse), sem)
     field[60:64, :] = jnp.zeros((4, NODES), F32)
-    field[0:60, :] = state_ref[...]
+    copies[0].wait()
+    field[0:60, :] = state[...]
     wp_ref[64:128, :] = field[...].astype(BF)
-    field[60:64, :] = jnp.zeros((4, NODES), F32)
-    field[0:60, :] = res_ref[...]
-    invert(field, inv_ref, value, None, None)
+    copies[1].wait()
+    field[0:60, :] = res[...]
+    copies[2].wait()
+    invert(field, inverse, value, None, None)
     w_ref[...] = value[0:60, :]
     pad_modes(value, padded, wp_ref)
 
@@ -243,9 +265,10 @@
 
 def along_body(slot_ref, core_ref, *refs):
     blocks = refs[0:8]
-    mine_ref, theirs_ref, cf, table_ref, w_ref, trace_ref = refs[8:14]
+    mine_ref, theirs_ref, cf, table_src, w_src, trace_src = refs[8:14]
     f_ref, toward_ref, onward_ref, grads_ref = refs[14:18]
-    picked, first_grads, sem = refs[18:21]
+    picked, first_grads, sem, table_ref, w_ref, trace_ref, late = refs[18:25]
+    copies = fetch((table_src, w_src, trace_src), (table_ref, w_ref, trace_ref), late)
     for stored in range(4):
         for index in range(8):
 
@@ -258,6 +281,7 @@
     for stored in range(4):
         pltpu.make_async_copy(blocks[0].at[0:64], picked.at[stored], sem.at[stored]).wait()
     core = core_ref[0]
+    copies[0].wait()
     for pair in range(8):
         tile = picked[:, :, 128 * pair : 128 * pair + 128].reshape(256, 128)
         values = dot(jnp.concatenate([tile, tile], axis=1), table_ref[...]).astype(BF)
@@ -277,6 +301,8 @@
         return carry
 
     lax.fori_loop(0, 2, step, 0)
+    copies[1].wait()
+    copies[2].wait()
     zero = jnp.zeros((4, 512), F32)
     for half in range(2):
         value = (LIFT_SCALE * PENALTY) * jnp.concatenate(
@@ -326,8 +352,8 @@
                 faces[face, 2 * pair + 1] = jnp.where(first, turned, mixed)
     near = []
     for element in range(16):
-        left = jnp.where(first, faces[0, ids_ref[element, 0]], faces[1, ids_ref[element, 1]])
-        right = jnp.where(first, faces[2, ids_ref[element, 2]], faces[3, ids_ref[element, 3]])
+        left = jnp.where(first, faces[0, ids_ref[0, element]], faces[1, ids_ref[1, element]])
+        right = jnp.where(first, faces[2, ids_ref[2, element]], faces[3, ids_ref[3, element]])
         high, low = split(jnp.concatenate([left, right], axis=1))
         near.append(dot(high, near_ref[...]) + dot(low, near_ref[...]))
     row = lax.broadcasted_iota(jnp.int32, (256, 128), 0)
@@ -338,8 +364,8 @@
     for pair in range(8):
         cols = slice(128 * pair, 128 * pair + 128)
         left, right = 2 * pair, 2 * pair + 1
-        below = 16 * jnp.where(column < 64, ids_ref[left, 4], ids_ref[right, 4]) + inner
-        above = 16 * jnp.where(column < 64, ids_ref[left, 5], ids_ref[right, 5]) + inner - 48
+        below = 16 * jnp.where(column < 64, ids_ref[4, left], ids_ref[4, right]) + inner
+        above = 16 * jnp.where(column < 64, ids_ref[5, left], ids_ref[5, right]) + inner - 48
         lower = jnp.where(row == jnp.where(inner < 16, below, -1), 1.0, 0.0).astype(BF)
         upper = jnp.where(row == jnp.where(inner >= 48, above, -1), 1.0, 0.0).astype(BF)
         across = dot(uh, lower) + dot(ul, lower) + dot(nh, upper) + dot(nl, upper)
@@ -408,6 +434,7 @@
     mode_rows = shaped((MB, NODES), F32)
     padded_rows = shaped((ROWS, NODES), BF)
     tile = pltpu.VMEM((ROWS, NODES), F32)
+    rows = pltpu.VMEM((MB, NODES), F32)
 
     (stored,) = call(
         stored_body,
@@ -420,26 +447,30 @@
     sent = jnp.broadcast_to(jnp.stack([stored, far]), (4, 2, PAIRS, 16, 128))
     held = lax.all_to_all(sent, "elem", 0, 0, axis_index_groups=groups)
     correction, padded = call(
-        start_body, (mode_rows, shaped((128, NODES), BF)), (VMEM,) * 3, (tile, tile, tile)
+        start_body,
+        (mode_rows, shaped((128, NODES), BF)),
+        (FAR,) * 3,
+        (tile, tile, tile, rows, tile, rows, pltpu.SemaphoreType.DMA((3,))),
     )(newton_residual, inverse_blocks, iterate)
     pieces = over_mode(padded)
 
-    lead = jnp.pad(basis_values[:, :K].T, ((0, 12), (0, 0)))
-    spread = jnp.pad(basis_values.reshape(S, 8, MB), ((0, 0), (0, 0), (0, 4))).reshape(S, 512)
-    held, spread, lead, slots, spots, ids = lax.optimization_barrier(
-        (held, spread, lead, slots, spots, neighbour_ids)
-    )
-    (mine,) = call(turn_body, (shaped((4, K, 16, 128), BF),), (SMEM,) + (VMEM,) * 2, ())(
-        side, held, jnp.asarray(np.eye(128), BF)
+    held, slots, spots, ids = lax.optimization_barrier((held, slots, spots, neighbour_ids.T))
+    (mine,) = call(turn_body, (shaped((4, K, 16, 128), BF),), (SMEM,) * 2 + (VMEM,) * 2, ())(
+        side, ids, held, jnp.asarray(np.eye(128), BF)
     )
     theirs = lax.ppermute(mine, "elem", pairs_of(16, lambda i: i ^ 1))
     (coeffs,) = call(
         coefficient_body,
         (shaped((2, 96, 512), F32),),
-        (SMEM,) + (ANY,) * 8 + (VMEM,) * 2,
-        (pltpu.VMEM((8, 64, NODES), BF), pltpu.SemaphoreType.DMA((8,))),
-    )(spots, *pieces, spread, lead)
-
+        (SMEM,) + (ANY,) * 9,
+        (
+            pltpu.VMEM((8, ROWS, NODES), BF),
+            pltpu.VMEM((480, NODES), F32),
+            pltpu.VMEM((480, S), BF),
+            pltpu.VMEM((S, 480), BF),
+            pltpu.SemaphoreType.DMA((9,)),
+        ),
+    )(spots, *pieces, basis_values.T)
 
     gradients_of = jnp.asarray(gradient_table())
     own = jnp.asarray(own_tables())
@@ -456,11 +487,15 @@
                 shaped((ROWS, 256), F32),
                 shaped((4, 16, 16, 512), BF),
             ),
-            (SMEM, SMEM) + (ANY,) * 8 + (VMEM,) * 6,
+            (SMEM, SMEM) + (ANY,) * 8 + (VMEM,) * 3 + (ANY,) * 3,
             (
                 pltpu.VMEM((4, ROWS, NODES), BF),
                 pltpu.VMEM((2, 16, 16, 512), BF),
                 pltpu.SemaphoreType.DMA((4,)),
+                pltpu.VMEM((256, 384), BF),
+                pltpu.VMEM((MB, NODES), F32),
+                pltpu.VMEM((2, 512, 128), BF),
+                pltpu.SemaphoreType.DMA((3,)),
             ),
         )(slots, core, *pieces, mine, theirs, coeffs, gradients_of, correction, traces)
         after = lax.ppermute(toward, "elem", pairs_of(16, lambda i: (i + 15) % 16))

time: 145 us -> 127 us (0.88)
  Pallas kernels: 57.2 us -> 39.4 us
  local copies, waits for them, and re-layouts: 9.31 us -> 5.82 us
  starting transfers between devices: 34.8 us -> 37.9 us
  waiting for transfers between devices: 40.3 us -> 42.5 us
  other arithmetic: 2.09 us -> 0.07 us
    pallas_call x2, Pallas kernels: 18.6 us -> 12.8 us  [per_device(): call(across_body, (shaped((4, ROWS, 512), BF),), (VMEM,) * 4, ())]
    pallas_call x3, Pallas kernels: 13.1 us -> 8.23 us  [the longest x1 5.61 us: per_device(): call(coefficient_body, (shaped((2, 96, 512), F32),), (SMEM,) + (ANY,) * 9...]
    ppermute x2, waiting for transfers between devices: 4.43 us -> 0.01 us  [over_mode(): two = lax.ppermute(block, 'mode', along(2))]
    ppermute x2, waiting for transfers between devices: 0.01 us -> 4.39 us  [over_mode(): three = lax.ppermute(block, 'mode', along(3))]
    ppermute x2, waiting for transfers between devices: 4 us -> 0.01 us  [over_mode(): lax.ppermute(two, 'mode', flip)]
    pallas_call x2, Pallas kernels: 16.1 us -> 12.4 us  [per_device(): call(along_body, (shaped((2, ROWS, 512), BF), shaped((ROWS, 256), F32), s...]
    all_to_all x1, waiting for transfers between devices: 14.9 us -> 18 us  [per_device(): held = lax.all_to_all(sent, 'elem', 0, 0, axis_index_groups=groups)]
    ppermute x2, starting transfers between devices: 8.27 us -> 10.7 us  [per_device(): after = lax.ppermute(toward, 'elem', pairs_of(16, lambda i: (i + 15) % 16))]
  transfers between devices with their start and end apart: 21 -> 21, of which waited for: 13 -> 10; matrix products, arithmetic and copies ran while one was open for 3% -> 0% of each run, Pallas kernels for 19% -> 15%
where the time goes in v1:
time: 127 us
  waiting for transfers between devices  42.5 us (33%)
  Pallas kernels  39.4 us (31%)
  starting transfers between devices  37.9 us (30%)
  local copies, waits for them, and re-layouts  5.82 us (5%)
    all_to_all x1, waiting for transfers between devices, per_device(): held = lax.all_to_all(sent, 'elem', 0, 0, axis_index_groups=groups)  18 us
    pallas_call x2, Pallas kernels, per_device(): call(across_body, (shaped((4, ROWS, 512), BF),), (VMEM,) * 4, ())  12.8 us
    pallas_call x2, Pallas kernels, per_device(): call(along_body, (shaped((2, ROWS, 512), BF), shaped((ROWS, 256), F32), s...  12.4 us
    ppermute x2, starting transfers between devices, per_device(): after = lax.ppermute(toward, 'elem', pairs_of(16, lambda i: (i + 15) % 16))  10.7 us
    ppermute x2, waiting for transfers between devices, over_mode(): lax.ppermute(other, 'mode', along(1))  7.01 us
    pallas_call x2, Pallas kernels, per_device(): call(update_body, (mode_rows, mode_rows, padded_rows), (SMEM,) + (VMEM,)...  5.66 us
    pallas_call x1, Pallas kernels, per_device(): call(coefficient_body, (shaped((2, 96, 512), F32),), (SMEM,) + (ANY,) * 9...  5.61 us
    all_to_all x1, starting transfers between devices, per_device(): held = lax.all_to_all(sent, 'elem', 0, 0, axis_index_groups=groups)  4.59 us
  transfers between devices with their start and end apart: 21, of which 10 were waited for; matrix products, arithmetic and copies ran while one was open for 0% of the time, Pallas kernels for 15%

profile of v1, /device:TPU:0, one launch (start us, length us, event | category | flops | bytes accessed | tf_op | source)
XLA Modules:
  0.0 126.6 jit_solution(156058833432644064)
XLA Ops:
  0.6 0.9 copy-done.13
  1.5 0.3 shard_map.140
  1.8 4.1 %collective-permute-start = (bf16[42,16,128]{2,1,0:T(8,128)(2,1)S(1)}, bf16[42,16,128]{2,1,0:T(8,128)(2,1)S(1)}, u32[]{:S(2)}, u32[]{:S(2)}) collective-permute-start(bf16[42,16,128]{2,1,0:T(8,128)(2,1)S(1)} %shard_map.140), channel_id=1, source_target_pairs={{0,64},{8,72},{16,80},{24,88},{32,96},{40,104},{48,112},{56,120},{... | collective-permute-start | bytes 516104 | tf_op jit(solution)/shard_map/ppermute | solution.py:445
  5.9 4.4 %collective-permute-done = bf16[42,16,128]{2,1,0:T(8,128)(2,1)S(1)} collective-permute-done((bf16[42,16,128]{2,1,0:T(8,128)(2,1)S(1)}, bf16[42,16,128]{2,1,0:T(8,128)(2,1)S(1)}, u32[]{:S(2)}, u32[]{:S(2)}) %collective-permute-start) | collective-permute-done | bytes 172064 | tf_op jit(solution)/shard_map/ppermute | solution.py:445
  10.3 1.3 %broadcast_in_dim.9 = bf16[4,2,42,16,128]{4,3,2,1,0:T(8,128)(2,1)} broadcast(bf16[2,42,16,128]{3,2,1,0:T(8,128)(2,1)S(1)} %pad_maximum_fusion), dimensions={1,2,3,4} | broadcast | bytes 1720320 | tf_op jit(solution)/shard_map/broadcast_in_dim | solution.py:447
  11.6 4.6 %all-to-all-start = ((bf16[4,2,42,16,128]{4,3,2,1,0:T(8,128)(2,1)}), bf16[4,2,42,16,128]{4,3,2,1,0:T(8,128)(2,1)S(1)}, u32[]{:S(2)}, u32[]{:S(2)}) async-start(bf16[4,2,42,16,128]{4,3,2,1,0:T(8,128)(2,1)} %broadcast_in_dim.9), calls=%async_computation | async-start | bytes 2752512 | tf_op jit(solution)/shard_map/all_to_all | solution.py:448
  16.3 18.0 %all-to-all-done.held = bf16[4,2,42,16,128]{4,3,2,1,0:T(8,128)(2,1)S(1)} async-done(((bf16[4,2,42,16,128]{4,3,2,1,0:T(8,128)(2,1)}), bf16[4,2,42,16,128]{4,3,2,1,0:T(8,128)(2,1)S(1)}, u32[]{:S(2)}, u32[]{:S(2)}) %all-to-all-start) | async-done | bytes 1376288 | tf_op jit(solution)/shard_map/all_to_all | solution.py:448
  34.3 0.0 copy-start.11
  34.3 2.1 %shard_map.142.refs_8_.mine_ref = bf16[4,84,16,128]{3,2,1,0:T(8,128)(2,1)S(1)} custom-call(s32[1]{0:T(128)} %bitcast.6.side_ref, s32[6,16]{1,0:T(8,128)S(1)} %bitcast.23, bf16[4,2,42,16,128]{4,3,2,1,0:T(8,128)(2,1)S(1)} %all-to-all-done.held, bf16[128,128]{1,0:T(8,128)(2,1)S(1)} %copy-done.15), custom_call_target="tpu_custom_call" | custom-call | tf_op jit(solution)/shard_map/pallas_call | solution.py:458
  36.4 0.1 collective-permute-start.8
  36.5 0.5 shard_map.141
  37.0 0.0 copy-start.5
  37.1 0.7 copy-done.5
  37.7 1.0 collective-permute-start.4
  38.8 2.8 %collective-permute-start.3 = (bf16[128,1024]{1,0:T(8,128)(2,1)S(1)}, bf16[128,1024]{1,0:T(8,128)(2,1)S(1)}, u32[]{:S(2)}, u32[]{:S(2)}) collective-permute-start(bf16[128,1024]{1,0:T(8,128)(2,1)S(1)} %get-tuple-element.23.refs_0_), channel_id=1, source_target_pairs={{0,6},{1,7},{2,0},{3,1},{4,2},{5,3},{6,4},{7,5},{8,14},{9,15},{10,... | collective-permute-start | bytes 786440 | tf_op jit(solution)/shard_map/ppermute | solution.py:404
  41.5 0.8 collective-permute-start.2
  42.3 0.9 collective-permute-start.1
  43.2 3.3 %collective-permute-done.4.refs_4_ = bf16[128,1024]{1,0:T(8,128)(2,1)} collective-permute-done((bf16[128,1024]{1,0:T(8,128)(2,1)S(1)}, bf16[128,1024]{1,0:T(8,128)(2,1)}, u32[]{:S(2)}, u32[]{:S(2)}) %collective-permute-start.4) | collective-permute-done | bytes 262176 | tf_op jit(solution)/shard_map/ppermute | solution.py:401
  46.5 2.8 %collective-permute-start.7 = (bf16[128,1024]{1,0:T(8,128)(2,1)}, bf16[128,1024]{1,0:T(8,128)(2,1)}, u32[]{:S(2)}, u32[]{:S(2)}) collective-permute-start(bf16[128,1024]{1,0:T(8,128)(2,1)} %collective-permute-done.4.refs_4_), channel_id=1, source_target_pairs={{0,6},{1,7},{2,0},{3,1},{4,2},{5,3},{6,4},{7,5},{8,14},{9,15},{10,... | collective-permute-start | bytes 786440 | tf_op jit(solution)/shard_map/ppermute | solution.py:413
  49.3 4.4 %collective-permute-done.3.refs_3_ = bf16[128,1024]{1,0:T(8,128)(2,1)S(1)} collective-permute-done((bf16[128,1024]{1,0:T(8,128)(2,1)S(1)}, bf16[128,1024]{1,0:T(8,128)(2,1)S(1)}, u32[]{:S(2)}, u32[]{:S(2)}) %collective-permute-start.3) | collective-permute-done | bytes 262176 | tf_op jit(solution)/shard_map/ppermute | solution.py:404
  53.7 0.7 copy-done.2
  54.4 0.0 collective-permute-start.5
  54.4 1.0 collective-permute-start.6
  55.4 1.4 %collective-permute-done.1.refs_1_ = bf16[128,1024]{1,0:T(8,128)(2,1)} collective-permute-done((bf16[128,1024]{1,0:T(8,128)(2,1)S(1)}, bf16[128,1024]{1,0:T(8,128)(2,1)}, u32[]{:S(2)}, u32[]{:S(2)}) %collective-permute-start.1) | collective-permute-done | bytes 262176 | tf_op jit(solution)/shard_map/ppermute | solution.py:402
  56.9 1.9 %collective-permute-done.7.refs_7_ = bf16[128,1024]{1,0:T(8,128)(2,1)} collective-permute-done((bf16[128,1024]{1,0:T(8,128)(2,1)}, bf16[128,1024]{1,0:T(8,128)(2,1)}, u32[]{:S(2)}, u32[]{:S(2)}) %collective-permute-start.7) | collective-permute-done | bytes 262176 | tf_op jit(solution)/shard_map/ppermute | solution.py:413
  58.8 4.6 %collective-permute-done.5.refs_5_ = bf16[128,1024]{1,0:T(8,128)(2,1)} collective-permute-done((bf16[128,1024]{1,0:T(8,128)(2,1)}, bf16[128,1024]{1,0:T(8,128)(2,1)}, u32[]{:S(2)}, u32[]{:S(2)}) %collective-permute-start.5) | collective-permute-done | bytes 262176 | tf_op jit(solution)/shard_map/ppermute | solution.py:411
  63.4 0.9 copy-done.3
  64.3 1.2 copy-done.8
  65.5 5.6 %shard_map.143.refs_10_.cf = f32[2,96,512]{2,1,0:T(8,128)S(1)} custom-call(s32[8]{0:T(128)S(1)} %fusion.5.spot_ref, bf16[128,1024]{1,0:T(8,128)(2,1)S(1)} %get-tuple-element.23.refs_0_, bf16[128,1024]{1,0:T(8,128)(2,1)} %collective-permute-done.1.refs_1_, bf16[128,1024]{1,0:T(8,128)(2,1)} %collective-permute-done.2.refs_2_, bf16[128,1024]{1,0:T(8,128)(2,1)S(1)} %copy-done.3, ...), custom_call_target="tpu_custom_call" | custom-call | tf_op jit(solution)/shard_map/pallas_call | solution.py:462
  71.2 6.3 %shard_map.144 = (bf16[2,64,512]{2,1,0:T(8,128)(2,1)S(1)}, f32[64,256]{1,0:T(8,128)S(1)}, f32[64,256]{1,0:T(8,128)S(1)}, bf16[4,16,16,512]{3,2,1,0:T(8,128)(2,1)S(1)}) custom-call(s32[4]{0:T(128)S(1)} %fusion.slot_ref, s32[1]{0:T(128)} %bitcast.5.core_ref, bf16[128,1024]{1,0:T(8,128)(2,1)S(1)} %get-tuple-element.23.refs_0_, ...), custom_call_target="tpu_custom_call" | custom-call | tf_op jit(solution)/shard_map/pallas_call | solution.py:482
  77.5 0.1 collective-permute-start.9
  77.6 5.3 %collective-permute-start.10 = (f32[64,256]{1,0:T(8,128)S(1)}, f32[64,256]{1,0:T(8,128)S(1)}, u32[]{:S(2)}, u32[]{:S(2)}) collective-permute-start(f32[64,256]{1,0:T(8,128)S(1)} %get-tuple-element.29), channel_id=1, source_target_pairs={{0,120},{8,0},{16,8},{24,16},{32,24},{40,32},{48,40},{56,48},{64,5... | collective-permute-start | bytes 196616 | tf_op jit(solution)/shard_map/ppermute | solution.py:501
  83.0 6.4 %shard_map.145.f_ref = bf16[4,64,512]{2,1,0:T(8,128)(2,1)S(1)} custom-call(bf16[4,84,16,128]{3,2,1,0:T(8,128)(2,1)S(1)} %shard_map.142.refs_8_.mine_ref, bf16[4,84,16,128]{3,2,1,0:T(8,128)(2,1)S(1)} %collective-permute-done.8.refs_9_.theirs_ref, f32[2,96,512]{2,1,0:T(8,128)S(1)} %shard_map.143.refs_10_.cf, ...), custom_call_target="tpu_custom_call" | custom-call | tf_op jit(solution)/shard_map/pallas_call | solution.py:503
  89.5 2.7 %shard_map.146 = (f32[60,1024]{1,0:T(8,128)}, f32[60,1024]{1,0:T(8,128)S(1)}, bf16[64,1024]{1,0:T(8,128)(2,1)S(1)}) custom-call(s32[6,16]{1,0:T(8,128)S(1)} %bitcast.24, f32[60,1024]{1,0:T(8,128)S(1)} %copy-done.6, bf16[2,64,512]{2,1,0:T(8,128)(2,1)S(1)} %get-tuple-element.26.fx_ref, bf16[4,64,512]{2,1,0:T(8,128)(2,1)S(1)} %shard_map.145.f_ref, ...), custom_call_target="tpu_custom_call" | custom-call | tf_op jit(solution)/shard_map/pallas_call | solution.py:506
  92.2 1.1 collective-permute-start.14
  93.3 3.0 %collective-permute-start.12 = (bf16[64,1024]{1,0:T(8,128)(2,1)S(1)}, bf16[64,1024]{1,0:T(8,128)(2,1)S(1)}, u32[]{:S(2)}, u32[]{:S(2)}) collective-permute-start(bf16[64,1024]{1,0:T(8,128)(2,1)S(1)} %get-tuple-element.31.refs_0_), channel_id=1, source_target_pairs={{0,4},{1,5},{2,6},{3,7},{4,0},{5,1},{6,2},{7,3},{8,12},{9,13},{10,... | collective-permute-start | bytes 393224 | tf_op jit(solution)/shard_map/ppermute | solution.py:403
  96.3 2.0 %collective-permute-start.11 = (bf16[64,1024]{1,0:T(8,128)(2,1)S(1)}, bf16[64,1024]{1,0:T(8,128)(2,1)S(1)}, u32[]{:S(2)}, u32[]{:S(2)}) collective-permute-start(bf16[64,1024]{1,0:T(8,128)(2,1)S(1)} %get-tuple-element.31.refs_0_), channel_id=1, source_target_pairs={{0,2},{1,3},{2,4},{3,5},{4,6},{5,7},{6,0},{7,1},{8,10},{9,11},{10,... | collective-permute-start | bytes 393224 | tf_op jit(solution)/shard_map/ppermute | solution.py:402
  98.3 1.2 collective-permute-start.17
  99.5 0.8 collective-permute-start.15
  100.3 0.9 collective-permute-start.16
  101.3 1.2 collective-permute-done.11.refs_1_
  102.5 0.8 collective-permute-done.17.refs_7_
  103.3 2.4 %collective-permute-done.15.refs_5_ = bf16[64,1024]{1,0:T(8,128)(2,1)S(1)} collective-permute-done((bf16[64,1024]{1,0:T(8,128)(2,1)S(1)}, bf16[64,1024]{1,0:T(8,128)(2,1)S(1)}, u32[]{:S(2)}, u32[]{:S(2)}) %collective-permute-start.15) | collective-permute-done | bytes 131104 | tf_op jit(solution)/shard_map/ppermute | solution.py:411
  105.7 6.1 %shard_map.147 = (bf16[2,64,512]{2,1,0:T(8,128)(2,1)S(1)}, f32[64,256]{1,0:T(8,128)S(1)}, f32[64,256]{1,0:T(8,128)S(1)}, bf16[4,16,16,512]{3,2,1,0:T(8,128)(2,1)S(1)}) custom-call(s32[4]{0:T(128)S(1)} %fusion.slot_ref, s32[1]{0:T(128)} %bitcast.5.core_ref, bf16[64,1024]{1,0:T(8,128)(2,1)S(1)} %get-tuple-element.31.refs_0_, ...), custom_call_target="tpu_custom_call" | custom-call | tf_op jit(solution)/shard_map/pallas_call | solution.py:482
  111.8 0.1 collective-permute-start.18
  111.9 5.3 %collective-permute-start.19 = (f32[64,256]{1,0:T(8,128)S(1)}, f32[64,256]{1,0:T(8,128)S(1)}, u32[]{:S(2)}, u32[]{:S(2)}) collective-permute-start(f32[64,256]{1,0:T(8,128)S(1)} %get-tuple-element.35), channel_id=1, source_target_pairs={{0,120},{8,0},{16,8},{24,16},{32,24},{40,32},{48,40},{56,48},{64,5... | collective-permute-start | bytes 196616 | tf_op jit(solution)/shard_map/ppermute | solution.py:501
  117.2 6.4 %shard_map.148.f_ref = bf16[4,64,512]{2,1,0:T(8,128)(2,1)S(1)} custom-call(bf16[4,84,16,128]{3,2,1,0:T(8,128)(2,1)S(1)} %shard_map.142.refs_8_.mine_ref, bf16[4,84,16,128]{3,2,1,0:T(8,128)(2,1)S(1)} %collective-permute-done.8.refs_9_.theirs_ref, f32[2,96,512]{2,1,0:T(8,128)S(1)} %shard_map.143.refs_10_.cf, ...), custom_call_target="tpu_custom_call" | custom-call | tf_op jit(solution)/shard_map/pallas_call | solution.py:503
  123.7 2.9 %shard_map.149 = (f32[60,1024]{1,0:T(8,128)}, f32[60,1024]{1,0:T(8,128)}, bf16[64,1024]{1,0:T(8,128)(2,1)}) custom-call(s32[6,16]{1,0:T(8,128)S(1)} %bitcast.25, f32[60,1024]{1,0:T(8,128)S(1)} %get-tuple-element.30.refs_12_.w_ref, bf16[2,64,512]{2,1,0:T(8,128)(2,1)S(1)} %get-tuple-element.32.fx_ref, bf16[4,64,512]{2,1,0:T(8,128)(2,1)S(1)} %shard_map.148.f_ref, ...), custom_call_target="tpu_custom_call" | custom-call | tf_op jit(solution)/shard_map/pallas_call | solution.py:506
  (44 shorter events, 0.2 us)
Async XLA Ops:
  0.6 0.9 copy-start.13
  1.8 8.4 %collective-permute-start = (bf16[42,16,128]{2,1,0:T(8,128)(2,1)S(1)}, bf16[42,16,128]{2,1,0:T(8,128)(2,1)S(1)}, u32[]{:S(2)}, u32[]{:S(2)}) collective-permute-start(bf16[42,16,128]{2,1,0:T(8,128)(2,1)S(1)} %shard_map.140), channel_id=1, source_target_pairs={{0,64},{8,72},{16,80},{24,88},{32,96},{40,104},{48,112},{56,120},{... | collective-permute-start | bytes 516104 | tf_op jit(solution)/shard_map/ppermute | solution.py:445
  11.6 4.6 %copy-start.17 = (s32[1,4]{1,0:T(1,128)S(1)}, s32[1,4]{1,0:T(1,128)}, u32[]{:S(2)}) copy-start(s32[1,4]{1,0:T(1,128)} %param.18) | copy-start | bytes 52
  11.6 22.6 %copy-start.14 = (s32[16,6]{0,1:T(8,128)S(1)}, s32[16,6]{0,1:T(8,128)}, u32[]{:S(2)}) copy-start(s32[16,6]{0,1:T(8,128)} %param.19) | copy-start | bytes 1156
  11.6 22.6 %copy-start.15 = (bf16[128,128]{1,0:T(8,128)(2,1)S(1)}, bf16[128,128]{1,0:T(8,128)(2,1)}, u32[]{:S(2)}) copy-start(bf16[128,128]{1,0:T(8,128)(2,1)} %constant.116.clone.eye_ref) | copy-start | bytes 98308
  11.6 22.6 %all-to-all-start = ((bf16[4,2,42,16,128]{4,3,2,1,0:T(8,128)(2,1)}), bf16[4,2,42,16,128]{4,3,2,1,0:T(8,128)(2,1)S(1)}, u32[]{:S(2)}, u32[]{:S(2)}) async-start(bf16[4,2,42,16,128]{4,3,2,1,0:T(8,128)(2,1)} %broadcast_in_dim.9), calls=%async_computation | async-start | bytes 2752512 | tf_op jit(solution)/shard_map/all_to_all | solution.py:448
  34.3 2.2 %copy-start = (f32[60,1024]{1,0:T(8,128)S(1)}, f32[60,1024]{1,0:T(8,128)}, u32[]{:S(2)}) copy-start(f32[60,1024]{1,0:T(8,128)} %res_ref.5) | copy-start | bytes 737284
  34.3 2.2 %copy-start.1 = (f32[64,1024]{1,0:T(8,128)S(1)}, f32[64,1024]{1,0:T(8,128)}, u32[]{:S(2)}) copy-start(f32[64,1024]{1,0:T(8,128)} %inv_ref.5) | copy-start | bytes 786436
  34.3 2.2 %copy-start.11 = (f32[60,1024]{1,0:T(8,128)S(1)}, f32[60,1024]{1,0:T(8,128)}, u32[]{:S(2)}) copy-start(f32[60,1024]{1,0:T(8,128)} %state_ref.1) | copy-start | bytes 737284
  36.4 34.8 %collective-permute-start.8 = (bf16[4,84,16,128]{3,2,1,0:T(8,128)(2,1)S(1)}, bf16[4,84,16,128]{3,2,1,0:T(8,128)(2,1)S(1)}, u32[]{:S(2)}, u32[]{:S(2)}) collective-permute-start(bf16[4,84,16,128]{3,2,1,0:T(8,128)(2,1)S(1)} %shard_map.142.refs_8_.mine_ref), channel_id=1, source_target_pairs={{0,8},{8,0},{16,24},{24,16},{32,40},{40,32},{48,56},{56,48},{64,72... | collective-permute-start | bytes 4128776 | tf_op jit(solution)/shard_map/ppermute | solution.py:461
  37.0 0.7 copy-start.5
  37.7 8.8 %collective-permute-start.4 = (bf16[128,1024]{1,0:T(8,128)(2,1)S(1)}, bf16[128,1024]{1,0:T(8,128)(2,1)}, u32[]{:S(2)}, u32[]{:S(2)}) collective-permute-start(bf16[128,1024]{1,0:T(8,128)(2,1)S(1)} %get-tuple-element.23.refs_0_), channel_id=1, source_target_pairs={{0,1},{1,0},{2,3},{3,2},{4,5},{5,4},{6,7},{7,6},{8,9},{9,8},{10,11... | collective-permute-start | bytes 786440 | tf_op jit(solution)/shard_map/ppermute | solution.py:401
  38.8 14.9 %collective-permute-start.3 = (bf16[128,1024]{1,0:T(8,128)(2,1)S(1)}, bf16[128,1024]{1,0:T(8,128)(2,1)S(1)}, u32[]{:S(2)}, u32[]{:S(2)}) collective-permute-start(bf16[128,1024]{1,0:T(8,128)(2,1)S(1)} %get-tuple-element.23.refs_0_), channel_id=1, source_target_pairs={{0,6},{1,7},{2,0},{3,1},{4,2},{5,3},{6,4},{7,5},{8,14},{9,15},{10,... | collective-permute-start | bytes 786440 | tf_op jit(solution)/shard_map/ppermute | solution.py:404
  41.5 12.9 %collective-permute-start.2 = (bf16[128,1024]{1,0:T(8,128)(2,1)S(1)}, bf16[128,1024]{1,0:T(8,128)(2,1)}, u32[]{:S(2)}, u32[]{:S(2)}) collective-permute-start(bf16[128,1024]{1,0:T(8,128)(2,1)S(1)} %get-tuple-element.23.refs_0_), channel_id=1, source_target_pairs={{0,4},{1,5},{2,6},{3,7},{4,0},{5,1},{6,2},{7,3},{8,12},{9,13},{10,... | collective-permute-start | bytes 786440 | tf_op jit(solution)/shard_map/ppermute | solution.py:403
  42.3 14.6 %collective-permute-start.1 = (bf16[128,1024]{1,0:T(8,128)(2,1)S(1)}, bf16[128,1024]{1,0:T(8,128)(2,1)}, u32[]{:S(2)}, u32[]{:S(2)}) collective-permute-start(bf16[128,1024]{1,0:T(8,128)(2,1)S(1)} %get-tuple-element.23.refs_0_), channel_id=1, source_target_pairs={{0,2},{1,3},{2,4},{3,5},{4,6},{5,7},{6,0},{7,1},{8,10},{9,11},{10,... | collective-permute-start | bytes 786440 | tf_op jit(solution)/shard_map/ppermute | solution.py:402
  46.5 12.2 %collective-permute-start.7 = (bf16[128,1024]{1,0:T(8,128)(2,1)}, bf16[128,1024]{1,0:T(8,128)(2,1)}, u32[]{:S(2)}, u32[]{:S(2)}) collective-permute-start(bf16[128,1024]{1,0:T(8,128)(2,1)} %collective-permute-done.4.refs_4_), channel_id=1, source_target_pairs={{0,6},{1,7},{2,0},{3,1},{4,2},{5,3},{6,4},{7,5},{8,14},{9,15},{10,... | collective-permute-start | bytes 786440 | tf_op jit(solution)/shard_map/ppermute | solution.py:413
  53.7 0.7 copy-start.2
  54.4 9.0 %collective-permute-start.5 = (bf16[128,1024]{1,0:T(8,128)(2,1)}, bf16[128,1024]{1,0:T(8,128)(2,1)}, u32[]{:S(2)}, u32[]{:S(2)}) collective-permute-start(bf16[128,1024]{1,0:T(8,128)(2,1)} %collective-permute-done.4.refs_4_), channel_id=1, source_target_pairs={{0,2},{1,3},{2,4},{3,5},{4,6},{5,7},{6,0},{7,1},{8,10},{9,11},{10,... | collective-permute-start | bytes 786440 | tf_op jit(solution)/shard_map/ppermute | solution.py:411
  54.4 9.0 %collective-permute-start.6 = (bf16[128,1024]{1,0:T(8,128)(2,1)}, bf16[128,1024]{1,0:T(8,128)(2,1)}, u32[]{:S(2)}, u32[]{:S(2)}) collective-permute-start(bf16[128,1024]{1,0:T(8,128)(2,1)} %collective-permute-done.2.refs_2_), channel_id=1, source_target_pairs={{0,1},{1,0},{2,3},{3,2},{4,5},{5,4},{6,7},{7,6},{8,9},{9,8},{10,11... | collective-permute-start | bytes 786440 | tf_op jit(solution)/shard_map/ppermute | solution.py:412
  63.4 1.0 copy-start.3
  64.3 1.2 copy-start.8
  65.5 5.6 %copy-start.4 = (bf16[128,1024]{1,0:T(8,128)(2,1)S(1)}, bf16[128,1024]{1,0:T(8,128)(2,1)}, u32[]{:S(2)}) copy-start(bf16[128,1024]{1,0:T(8,128)(2,1)} %copy-done.2) | copy-start | bytes 786436
  65.5 5.6 %copy-start.6 = (f32[60,1024]{1,0:T(8,128)S(1)}, f32[60,1024]{1,0:T(8,128)}, u32[]{:S(2)}) copy-start(f32[60,1024]{1,0:T(8,128)} %copy-done.5) | copy-start | bytes 737284
  65.5 5.7 %copy-start.7 = (bf16[2,512,128]{2,1,0:T(8,128)(2,1)S(1)}, bf16[2,512,128]{2,1,0:T(8,128)(2,1)}, u32[]{:S(2)}) copy-start(bf16[2,512,128]{2,1,0:T(8,128)(2,1)} %constant.120.clone.refs_13_) | copy-start | bytes 786436
  65.5 5.7 %copy-start.9 = (bf16[256,384]{1,0:T(8,128)(2,1)S(1)}, bf16[256,384]{1,0:T(8,128)(2,1)}, u32[]{:S(2)}) copy-start(bf16[256,384]{1,0:T(8,128)(2,1)} %constant.117.clone.refs_11_) | copy-start | bytes 589828
  77.5 11.9 %collective-permute-start.9 = (f32[64,256]{1,0:T(8,128)S(1)}, f32[64,256]{1,0:T(8,128)S(1)}, u32[]{:S(2)}, u32[]{:S(2)}) collective-permute-start(f32[64,256]{1,0:T(8,128)S(1)} %get-tuple-element.28), channel_id=1, source_target_pairs={{0,8},{8,16},{16,24},{24,32},{32,40},{40,48},{48,56},{56,64},{64,7... | collective-permute-start | bytes 196616 | tf_op jit(solution)/shard_map/ppermute | solution.py:502
  77.6 11.8 %collective-permute-start.10 = (f32[64,256]{1,0:T(8,128)S(1)}, f32[64,256]{1,0:T(8,128)S(1)}, u32[]{:S(2)}, u32[]{:S(2)}) collective-permute-start(f32[64,256]{1,0:T(8,128)S(1)} %get-tuple-element.29), channel_id=1, source_target_pairs={{0,120},{8,0},{16,8},{24,16},{32,24},{40,32},{48,40},{56,48},{64,5... | collective-permute-start | bytes 196616 | tf_op jit(solution)/shard_map/ppermute | solution.py:501
  83.0 6.5 %copy-start.10 = (bf16[2,384,128]{2,1,0:T(8,128)(2,1)S(1)}, bf16[2,384,128]{2,1,0:T(8,128)(2,1)}, u32[]{:S(2)}) copy-start(bf16[2,384,128]{2,1,0:T(8,128)(2,1)} %constant.118.clone.own_ref) | copy-start | bytes 589828
  83.0 6.5 %copy-start.12 = (bf16[256,128]{1,0:T(8,128)(2,1)S(1)}, bf16[256,128]{1,0:T(8,128)(2,1)}, u32[]{:S(2)}) copy-start(bf16[256,128]{1,0:T(8,128)(2,1)} %constant.119.clone.near_ref) | copy-start | bytes 196612
  83.0 6.5 %copy-start.16 = (f32[1,128]{1,0:T(1,128)S(1)}, f32[1,128]{1,0:T(1,128)}, u32[]{:S(2)}) copy-start(f32[1,128]{1,0:T(1,128)} %constant.121.clone.count_ref) | copy-start | bytes 1540
  92.2 6.1 %collective-permute-start.14 = (bf16[64,1024]{1,0:T(8,128)(2,1)S(1)}, bf16[64,1024]{1,0:T(8,128)(2,1)S(1)}, u32[]{:S(2)}, u32[]{:S(2)}) collective-permute-start(bf16[64,1024]{1,0:T(8,128)(2,1)S(1)} %get-tuple-element.31.refs_0_), channel_id=1, source_target_pairs={{0,1},{1,0},{2,3},{3,2},{4,5},{5,4},{6,7},{7,6},{8,9},{9,8},{10,11... | collective-permute-start | bytes 393224 | tf_op jit(solution)/shard_map/ppermute | solution.py:401
  93.3 7.1 %collective-permute-start.12 = (bf16[64,1024]{1,0:T(8,128)(2,1)S(1)}, bf16[64,1024]{1,0:T(8,128)(2,1)S(1)}, u32[]{:S(2)}, u32[]{:S(2)}) collective-permute-start(bf16[64,1024]{1,0:T(8,128)(2,1)S(1)} %get-tuple-element.31.refs_0_), channel_id=1, source_target_pairs={{0,4},{1,5},{2,6},{3,7},{4,0},{5,1},{6,2},{7,3},{8,12},{9,13},{10,... | collective-permute-start | bytes 393224 | tf_op jit(solution)/shard_map/ppermute | solution.py:403
  96.3 5.0 %collective-permute-start.13 = (bf16[64,1024]{1,0:T(8,128)(2,1)S(1)}, bf16[64,1024]{1,0:T(8,128)(2,1)S(1)}, u32[]{:S(2)}, u32[]{:S(2)}) collective-permute-start(bf16[64,1024]{1,0:T(8,128)(2,1)S(1)} %get-tuple-element.31.refs_0_), channel_id=1, source_target_pairs={{0,6},{1,7},{2,0},{3,1},{4,2},{5,3},{6,4},{7,5},{8,14},{9,15},{10,... | collective-permute-start | bytes 393224 | tf_op jit(solution)/shard_map/ppermute | solution.py:404
  96.3 6.2 %collective-permute-start.11 = (bf16[64,1024]{1,0:T(8,128)(2,1)S(1)}, bf16[64,1024]{1,0:T(8,128)(2,1)S(1)}, u32[]{:S(2)}, u32[]{:S(2)}) collective-permute-start(bf16[64,1024]{1,0:T(8,128)(2,1)S(1)} %get-tuple-element.31.refs_0_), channel_id=1, source_target_pairs={{0,2},{1,3},{2,4},{3,5},{4,6},{5,7},{6,0},{7,1},{8,10},{9,11},{10,... | collective-permute-start | bytes 393224 | tf_op jit(solution)/shard_map/ppermute | solution.py:402
  98.3 5.0 %collective-permute-start.17 = (bf16[64,1024]{1,0:T(8,128)(2,1)S(1)}, bf16[64,1024]{1,0:T(8,128)(2,1)S(1)}, u32[]{:S(2)}, u32[]{:S(2)}) collective-permute-start(bf16[64,1024]{1,0:T(8,128)(2,1)S(1)} %collective-permute-done.14.refs_4_), channel_id=1, source_target_pairs={{0,6},{1,7},{2,0},{3,1},{4,2},{5,3},{6,4},{7,5},{8,14},{9,15},{10,... | collective-permute-start | bytes 393224 | tf_op jit(solution)/shard_map/ppermute | solution.py:413
  99.5 6.2 %collective-permute-start.15 = (bf16[64,1024]{1,0:T(8,128)(2,1)S(1)}, bf16[64,1024]{1,0:T(8,128)(2,1)S(1)}, u32[]{:S(2)}, u32[]{:S(2)}) collective-permute-start(bf16[64,1024]{1,0:T(8,128)(2,1)S(1)} %collective-permute-done.14.refs_4_), channel_id=1, source_target_pairs={{0,2},{1,3},{2,4},{3,5},{4,6},{5,7},{6,0},{7,1},{8,10},{9,11},{10,... | collective-permute-start | bytes 393224 | tf_op jit(solution)/shard_map/ppermute | solution.py:411
  100.3 5.4 %collective-permute-start.16 = (bf16[64,1024]{1,0:T(8,128)(2,1)S(1)}, bf16[64,1024]{1,0:T(8,128)(2,1)S(1)}, u32[]{:S(2)}, u32[]{:S(2)}) collective-permute-start(bf16[64,1024]{1,0:T(8,128)(2,1)S(1)} %collective-permute-done.12.refs_2_), channel_id=1, source_target_pairs={{0,1},{1,0},{2,3},{3,2},{4,5},{5,4},{6,7},{7,6},{8,9},{9,8},{10,11... | collective-permute-start | bytes 393224 | tf_op jit(solution)/shard_map/ppermute | solution.py:412
  111.8 11.9 %collective-permute-start.18 = (f32[64,256]{1,0:T(8,128)S(1)}, f32[64,256]{1,0:T(8,128)S(1)}, u32[]{:S(2)}, u32[]{:S(2)}) collective-permute-start(f32[64,256]{1,0:T(8,128)S(1)} %get-tuple-element.34), channel_id=1, source_target_pairs={{0,8},{8,16},{16,24},{24,32},{32,40},{40,48},{48,56},{56,64},{64,7... | collective-permute-start | bytes 196616 | tf_op jit(solution)/shard_map/ppermute | solution.py:502
  111.9 11.8 %collective-permute-start.19 = (f32[64,256]{1,0:T(8,128)S(1)}, f32[64,256]{1,0:T(8,128)S(1)}, u32[]{:S(2)}, u32[]{:S(2)}) collective-permute-start(f32[64,256]{1,0:T(8,128)S(1)} %get-tuple-element.35), channel_id=1, source_target_pairs={{0,120},{8,0},{16,8},{24,16},{32,24},{40,32},{48,40},{56,48},{64,5... | collective-permute-start | bytes 196616 | tf_op jit(solution)/shard_map/ppermute | solution.py:501

commit v2 on v1

--- a/solution.py
+++ b/solution.py
@@ -165,8 +165,11 @@
         z_ref[pair] = tall[pl.ds(2 * pair, 16, stride=K), :].astype(BF)
 
 
-def turn_body(side_ref, ids_ref, held, eye_ref, tt_ref):
+def turn_body(side_ref, ids_ref, held, tt_ref):
     side = side_ref[0]
+    place_row = lax.broadcasted_iota(jnp.int32, (128, 128), 0)
+    place_column = lax.broadcasted_iota(jnp.int32, (128, 128), 1)
+    eye = jnp.where(place_row == place_column, 1.0, 0.0).astype(BF)
 
     def step(twin, carry):
         rows = []
@@ -175,7 +178,7 @@
             rows.append(held[place % 4, zone, pl.ds(2 * twin, 2)])
         both = jnp.concatenate([row[pair] for pair in range(2) for row in rows], axis=0)
         turned = lax.dot_general(
-            eye_ref[...], both, (((1,), (1,)), ((), ())), preferred_element_type=F32
+            eye, both, (((1,), (1,)), ((), ())), preferred_element_type=F32
         ).astype(BF)
         for pair in range(2):
             for half in range(2):
@@ -410,7 +413,7 @@
         other,
         lax.ppermute(other, "mode", along(1)),
         lax.ppermute(two, "mode", flip),
-        lax.ppermute(other, "mode", along(3)),
+        lax.ppermute(three, "mode", flip),
     ]
 
 
@@ -451,12 +454,13 @@
         (mode_rows, shaped((128, NODES), BF)),
         (FAR,) * 3,
         (tile, tile, tile, rows, tile, rows, pltpu.SemaphoreType.DMA((3,))),
+        56 << 20,
     )(newton_residual, inverse_blocks, iterate)
     pieces = over_mode(padded)
 
     held, slots, spots, ids = lax.optimization_barrier((held, slots, spots, neighbour_ids.T))
-    (mine,) = call(turn_body, (shaped((4, K, 16, 128), BF),), (SMEM,) * 2 + (VMEM,) * 2, ())(
-        side, ids, held, jnp.asarray(np.eye(128), BF)
+    (mine,) = call(turn_body, (shaped((4, K, 16, 128), BF),), (SMEM,) * 2 + (VMEM,), ())(
+        side, ids, held
     )
     theirs = lax.ppermute(mine, "elem", pairs_of(16, lambda i: i ^ 1))
     (coeffs,) = call(

time: 127 us -> 135 us (1.063)
  waiting for transfers between devices: 42.5 us -> 48.4 us
  Pallas kernels: 39.4 us -> 41.7 us
  local copies, waits for them, and re-layouts: 5.82 us -> 4.4 us
    ppermute x2, waiting for transfers between devices: 0.01 us -> 6.37 us  [over_mode(): lax.ppermute(two, 'mode', flip)]
    ppermute x2, starting transfers between devices: 2.76 us -> 6.6 us  [over_mode(): three = lax.ppermute(block, 'mode', along(3))]
    ppermute x2, starting transfers between devices: 0.82 us -> 4.13 us  [over_mode(): lax.ppermute(other, 'mode', along(1))]
    ppermute x2, starting transfers between devices: 3.81 us -> 0.81 us  [over_mode(): two = lax.ppermute(block, 'mode', along(2))]
    ppermute x2, waiting for transfers between devices: 2.73 us -> 0.01 us  [over_mode(): lax.ppermute(three, 'mode', flip)]
    ppermute x2, starting transfers between devices: 3.97 us -> 1.93 us  [over_mode(): lax.ppermute(three, 'mode', flip)]
    pallas_call x1, Pallas kernels: 0.52 us -> 2.29 us  [per_device(): call(start_body, (mode_rows, shaped((128, NODES), BF)), (FAR,) * 3, (tile...]
    ppermute x2, waiting for transfers between devices: 0.01 us -> 1.74 us  [over_mode(): two = lax.ppermute(block, 'mode', along(2))]
  transfers between devices with their start and end apart: 21 -> 21, of which waited for: 10 -> 12; matrix products, arithmetic and copies ran while one was open for 0% -> 0% of each run, Pallas kernels for 15% -> 16%
where the time goes in v2:
time: 135 us; the launch traced here: 134 us
  waiting for transfers between devices  48.4 us (36%)
  Pallas kernels  41.7 us (31%)
  starting transfers between devices  38.9 us (29%)
  local copies, waits for them, and re-layouts  4.4 us (3%)
    all_to_all x1, waiting for transfers between devices, per_device(): held = lax.all_to_all(sent, 'elem', 0, 0, axis_index_groups=groups)  18 us
    pallas_call x2, Pallas kernels, per_device(): call(across_body, (shaped((4, ROWS, 512), BF),), (VMEM,) * 4, ())  12.8 us
    pallas_call x2, Pallas kernels, per_device(): call(along_body, (shaped((2, ROWS, 512), BF), shaped((ROWS, 256), F32), s...  12.6 us
    ppermute x2, starting transfers between devices, per_device(): after = lax.ppermute(toward, 'elem', pairs_of(16, lambda i: (i + 15) % 16))  10.7 us
    ppermute x2, waiting for transfers between devices, over_mode(): lax.ppermute(other, 'mode', along(1))  6.93 us
    ppermute x2, starting transfers between devices, over_mode(): three = lax.ppermute(block, 'mode', along(3))  6.6 us
    ppermute x2, waiting for transfers between devices, over_mode(): lax.ppermute(two, 'mode', flip)  6.37 us
    pallas_call x1, Pallas kernels, per_device(): call(coefficient_body, (shaped((2, 96, 512), F32),), (SMEM,) + (ANY,) * 9...  5.89 us
  transfers between devices with their start and end apart: 21, of which 12 were waited for; matrix products, arithmetic and copies ran while one was open for 0% of the time, Pallas kernels for 16%

profile of v2, /device:TPU:0, one launch (start us, length us, event | category | flops | bytes accessed | tf_op | source)
XLA Modules:
  0.0 134.3 jit_solution(13133508038643879555)
XLA Ops:
  0.6 0.9 copy-done.10
  1.5 0.3 shard_map.131
  1.8 4.1 %collective-permute-start = (bf16[42,16,128]{2,1,0:T(8,128)(2,1)S(1)}, bf16[42,16,128]{2,1,0:T(8,128)(2,1)S(1)}, u32[]{:S(2)}, u32[]{:S(2)}) collective-permute-start(bf16[42,16,128]{2,1,0:T(8,128)(2,1)S(1)} %shard_map.131), channel_id=1, source_target_pairs={{0,64},{8,72},{16,80},{24,88},{32,96},{40,104},{48,112},{56,120},{... | collective-permute-start | bytes 516104 | tf_op jit(solution)/shard_map/ppermute | solution.py:448
  5.9 4.4 %collective-permute-done = bf16[42,16,128]{2,1,0:T(8,128)(2,1)S(1)} collective-permute-done((bf16[42,16,128]{2,1,0:T(8,128)(2,1)S(1)}, bf16[42,16,128]{2,1,0:T(8,128)(2,1)S(1)}, u32[]{:S(2)}, u32[]{:S(2)}) %collective-permute-start) | collective-permute-done | bytes 172064 | tf_op jit(solution)/shard_map/ppermute | solution.py:448
  10.3 1.3 broadcast_in_dim.9
  11.6 4.6 %all-to-all-start = ((bf16[4,2,42,16,128]{4,3,2,1,0:T(8,128)(2,1)}), bf16[4,2,42,16,128]{4,3,2,1,0:T(8,128)(2,1)S(1)}, u32[]{:S(2)}, u32[]{:S(2)}) async-start(bf16[4,2,42,16,128]{4,3,2,1,0:T(8,128)(2,1)} %broadcast_in_dim.9), calls=%async_computation | async-start | bytes 2752512 | tf_op jit(solution)/shard_map/all_to_all | solution.py:451
  16.2 18.0 %all-to-all-done.held = bf16[4,2,42,16,128]{4,3,2,1,0:T(8,128)(2,1)S(1)} async-done(((bf16[4,2,42,16,128]{4,3,2,1,0:T(8,128)(2,1)}), bf16[4,2,42,16,128]{4,3,2,1,0:T(8,128)(2,1)S(1)}, u32[]{:S(2)}, u32[]{:S(2)}) %all-to-all-start) | async-done | bytes 1376288 | tf_op jit(solution)/shard_map/all_to_all | solution.py:451
  34.2 2.1 %shard_map.133.refs_8_.mine_ref = bf16[4,84,16,128]{3,2,1,0:T(8,128)(2,1)S(1)} custom-call(s32[1]{0:T(128)} %bitcast.6.side_ref, s32[6,16]{1,0:T(8,128)S(1)} %bitcast.23, bf16[4,2,42,16,128]{4,3,2,1,0:T(8,128)(2,1)S(1)} %all-to-all-done.held), custom_call_target="tpu_custom_call" | custom-call | tf_op jit(solution)/shard_map/pallas_call | solution.py:462
  36.4 0.1 collective-permute-start.8
  36.5 2.3 %shard_map.132 = (f32[60,1024]{1,0:T(8,128)}, bf16[128,1024]{1,0:T(8,128)(2,1)}) custom-call(f32[60,1024]{1,0:T(8,128)} %res_ref.5, f32[64,1024]{1,0:T(8,128)} %inv_ref.5, f32[60,1024]{1,0:T(8,128)} %state_ref.1), custom_call_target="tpu_custom_call" | custom-call | tf_op jit(solution)/shard_map/pallas_call | solution.py:452
  38.8 1.1 collective-permute-start.4
  39.8 2.8 %collective-permute-start.3 = (bf16[128,1024]{1,0:T(8,128)(2,1)}, bf16[128,1024]{1,0:T(8,128)(2,1)S(1)}, u32[]{:S(2)}, u32[]{:S(2)}) collective-permute-start(bf16[128,1024]{1,0:T(8,128)(2,1)} %get-tuple-element.23.refs_0_), channel_id=1, source_target_pairs={{0,6},{1,7},{2,0},{3,1},{4,2},{5,3},{6,4},{7,5},{8,14},{9,15},{10,... | collective-permute-start | bytes 786440 | tf_op jit(solution)/shard_map/ppermute | solution.py:407
  42.6 0.8 collective-permute-start.2
  43.4 0.9 collective-permute-start.1
  44.3 3.5 %collective-permute-done.4.refs_4_ = bf16[128,1024]{1,0:T(8,128)(2,1)S(1)} collective-permute-done((bf16[128,1024]{1,0:T(8,128)(2,1)}, bf16[128,1024]{1,0:T(8,128)(2,1)S(1)}, u32[]{:S(2)}, u32[]{:S(2)}) %collective-permute-start.4) | collective-permute-done | bytes 262176 | tf_op jit(solution)/shard_map/ppermute | solution.py:404
  47.8 1.5 %collective-permute-start.5 = (bf16[128,1024]{1,0:T(8,128)(2,1)S(1)}, bf16[128,1024]{1,0:T(8,128)(2,1)}, u32[]{:S(2)}, u32[]{:S(2)}) collective-permute-start(bf16[128,1024]{1,0:T(8,128)(2,1)S(1)} %collective-permute-done.4.refs_4_), channel_id=1, source_target_pairs={{0,2},{1,3},{2,4},{3,5},{4,6},{5,7},{6,0},{7,1},{8,10},{9,11},{10,... | collective-permute-start | bytes 786440 | tf_op jit(solution)/shard_map/ppermute | solution.py:414
  49.3 5.3 %collective-permute-done.3.refs_3_ = bf16[128,1024]{1,0:T(8,128)(2,1)S(1)} collective-permute-done((bf16[128,1024]{1,0:T(8,128)(2,1)}, bf16[128,1024]{1,0:T(8,128)(2,1)S(1)}, u32[]{:S(2)}, u32[]{:S(2)}) %collective-permute-start.3) | collective-permute-done | bytes 262176 | tf_op jit(solution)/shard_map/ppermute | solution.py:407
  54.5 1.0 collective-permute-start.7
  55.5 1.0 collective-permute-start.6
  56.5 1.7 %collective-permute-done.1.refs_1_ = bf16[128,1024]{1,0:T(8,128)(2,1)} collective-permute-done((bf16[128,1024]{1,0:T(8,128)(2,1)}, bf16[128,1024]{1,0:T(8,128)(2,1)}, u32[]{:S(2)}, u32[]{:S(2)}) %collective-permute-start.1) | collective-permute-done | bytes 262176 | tf_op jit(solution)/shard_map/ppermute | solution.py:405
  58.3 5.5 %collective-permute-done.5.refs_5_ = bf16[128,1024]{1,0:T(8,128)(2,1)} collective-permute-done((bf16[128,1024]{1,0:T(8,128)(2,1)S(1)}, bf16[128,1024]{1,0:T(8,128)(2,1)}, u32[]{:S(2)}, u32[]{:S(2)}) %collective-permute-start.5) | collective-permute-done | bytes 262176 | tf_op jit(solution)/shard_map/ppermute | solution.py:414
  63.8 3.8 %collective-permute-done.6.refs_6_ = bf16[128,1024]{1,0:T(8,128)(2,1)} collective-permute-done((bf16[128,1024]{1,0:T(8,128)(2,1)S(1)}, bf16[128,1024]{1,0:T(8,128)(2,1)}, u32[]{:S(2)}, u32[]{:S(2)}) %collective-permute-start.6) | collective-permute-done | bytes 262176 | tf_op jit(solution)/shard_map/ppermute | solution.py:415
  67.6 0.9 copy-done.2
  68.6 1.2 copy-done.6
  69.8 5.9 %shard_map.134.refs_10_.cf = f32[2,96,512]{2,1,0:T(8,128)S(1)} custom-call(s32[8]{0:T(128)S(1)} %fusion.5.spot_ref, bf16[128,1024]{1,0:T(8,128)(2,1)S(1)} %copy-done.2, bf16[128,1024]{1,0:T(8,128)(2,1)} %collective-permute-done.1.refs_1_, bf16[128,1024]{1,0:T(8,128)(2,1)S(1)} %collective-permute-done.2.refs_2_, ...), custom_call_target="tpu_custom_call" | custom-call | tf_op jit(solution)/shard_map/pallas_call | solution.py:466
  75.7 6.5 %shard_map.135 = (bf16[2,64,512]{2,1,0:T(8,128)(2,1)S(1)}, f32[64,256]{1,0:T(8,128)S(1)}, f32[64,256]{1,0:T(8,128)S(1)}, bf16[4,16,16,512]{3,2,1,0:T(8,128)(2,1)S(1)}) custom-call(s32[4]{0:T(128)S(1)} %fusion.slot_ref, s32[1]{0:T(128)} %bitcast.5.core_ref, bf16[128,1024]{1,0:T(8,128)(2,1)S(1)} %copy-done.3, ...), custom_call_target="tpu_custom_call" | custom-call | tf_op jit(solution)/shard_map/pallas_call | solution.py:486
  82.3 0.1 collective-permute-start.9
  82.3 5.3 %collective-permute-start.10 = (f32[64,256]{1,0:T(8,128)S(1)}, f32[64,256]{1,0:T(8,128)S(1)}, u32[]{:S(2)}, u32[]{:S(2)}) collective-permute-start(f32[64,256]{1,0:T(8,128)S(1)} %get-tuple-element.29), channel_id=1, source_target_pairs={{0,120},{8,0},{16,8},{24,16},{32,24},{40,32},{48,40},{56,48},{64,5... | collective-permute-start | bytes 196616 | tf_op jit(solution)/shard_map/ppermute | solution.py:505
  87.7 0.0 copy-start.12
  87.7 6.4 %shard_map.136.f_ref = bf16[4,64,512]{2,1,0:T(8,128)(2,1)S(1)} custom-call(bf16[4,84,16,128]{3,2,1,0:T(8,128)(2,1)S(1)} %shard_map.133.refs_8_.mine_ref, bf16[4,84,16,128]{3,2,1,0:T(8,128)(2,1)S(1)} %collective-permute-done.8.refs_9_.theirs_ref, f32[2,96,512]{2,1,0:T(8,128)S(1)} %shard_map.134.refs_10_.cf, ...), custom_call_target="tpu_custom_call" | custom-call | tf_op jit(solution)/shard_map/pallas_call | solution.py:507
  94.1 0.0 collective-permute-done.9.up_ref
  94.2 2.7 %shard_map.137 = (f32[60,1024]{1,0:T(8,128)}, f32[60,1024]{1,0:T(8,128)S(1)}, bf16[64,1024]{1,0:T(8,128)(2,1)S(1)}) custom-call(s32[6,16]{1,0:T(8,128)S(1)} %bitcast.24, f32[60,1024]{1,0:T(8,128)S(1)} %copy-done.4, bf16[2,64,512]{2,1,0:T(8,128)(2,1)S(1)} %get-tuple-element.26.fx_ref, bf16[4,64,512]{2,1,0:T(8,128)(2,1)S(1)} %shard_map.136.f_ref, ...), custom_call_target="tpu_custom_call" | custom-call | tf_op jit(solution)/shard_map/pallas_call | solution.py:510
  96.9 1.1 collective-permute-start.14
  98.0 3.8 %collective-permute-start.13 = (bf16[64,1024]{1,0:T(8,128)(2,1)S(1)}, bf16[64,1024]{1,0:T(8,128)(2,1)S(1)}, u32[]{:S(2)}, u32[]{:S(2)}) collective-permute-start(bf16[64,1024]{1,0:T(8,128)(2,1)S(1)} %get-tuple-element.31.refs_0_), channel_id=1, source_target_pairs={{0,6},{1,7},{2,0},{3,1},{4,2},{5,3},{6,4},{7,5},{8,14},{9,15},{10,... | collective-permute-start | bytes 393224 | tf_op jit(solution)/shard_map/ppermute | solution.py:407
  101.9 0.9 collective-permute-start.11
  102.7 2.6 %collective-permute-start.15 = (bf16[64,1024]{1,0:T(8,128)(2,1)S(1)}, bf16[64,1024]{1,0:T(8,128)(2,1)S(1)}, u32[]{:S(2)}, u32[]{:S(2)}) collective-permute-start(bf16[64,1024]{1,0:T(8,128)(2,1)S(1)} %collective-permute-done.14.refs_4_), channel_id=1, source_target_pairs={{0,2},{1,3},{2,4},{3,5},{4,6},{5,7},{6,0},{7,1},{8,10},{9,11},{10,... | collective-permute-start | bytes 393224 | tf_op jit(solution)/shard_map/ppermute | solution.py:414
  105.3 0.4 collective-permute-done.13.refs_3_
  105.8 0.9 collective-permute-start.17
  106.7 1.7 %collective-permute-done.12.refs_2_ = bf16[64,1024]{1,0:T(8,128)(2,1)S(1)} collective-permute-done((bf16[64,1024]{1,0:T(8,128)(2,1)S(1)}, bf16[64,1024]{1,0:T(8,128)(2,1)S(1)}, u32[]{:S(2)}, u32[]{:S(2)}) %collective-permute-start.12) | collective-permute-done | bytes 131104 | tf_op jit(solution)/shard_map/ppermute | solution.py:406
  108.4 0.9 collective-permute-start.16
  109.3 0.1 collective-permute-done.11.refs_1_
  109.4 1.4 %collective-permute-done.15.refs_5_ = bf16[64,1024]{1,0:T(8,128)(2,1)S(1)} collective-permute-done((bf16[64,1024]{1,0:T(8,128)(2,1)S(1)}, bf16[64,1024]{1,0:T(8,128)(2,1)S(1)}, u32[]{:S(2)}, u32[]{:S(2)}) %collective-permute-start.15) | collective-permute-done | bytes 131104 | tf_op jit(solution)/shard_map/ppermute | solution.py:414
  110.8 2.5 %collective-permute-done.16.refs_6_ = bf16[64,1024]{1,0:T(8,128)(2,1)S(1)} collective-permute-done((bf16[64,1024]{1,0:T(8,128)(2,1)S(1)}, bf16[64,1024]{1,0:T(8,128)(2,1)S(1)}, u32[]{:S(2)}, u32[]{:S(2)}) %collective-permute-start.16) | collective-permute-done | bytes 131104 | tf_op jit(solution)/shard_map/ppermute | solution.py:415
  113.4 6.1 %shard_map.138 = (bf16[2,64,512]{2,1,0:T(8,128)(2,1)S(1)}, f32[64,256]{1,0:T(8,128)S(1)}, f32[64,256]{1,0:T(8,128)S(1)}, bf16[4,16,16,512]{3,2,1,0:T(8,128)(2,1)S(1)}) custom-call(s32[4]{0:T(128)S(1)} %fusion.slot_ref, s32[1]{0:T(128)} %bitcast.5.core_ref, bf16[64,1024]{1,0:T(8,128)(2,1)S(1)} %get-tuple-element.31.refs_0_, ...), custom_call_target="tpu_custom_call" | custom-call | tf_op jit(solution)/shard_map/pallas_call | solution.py:486
  119.5 0.1 collective-permute-start.18
  119.6 5.3 %collective-permute-start.19 = (f32[64,256]{1,0:T(8,128)S(1)}, f32[64,256]{1,0:T(8,128)S(1)}, u32[]{:S(2)}, u32[]{:S(2)}) collective-permute-start(f32[64,256]{1,0:T(8,128)S(1)} %get-tuple-element.35), channel_id=1, source_target_pairs={{0,120},{8,0},{16,8},{24,16},{32,24},{40,32},{48,40},{56,48},{64,5... | collective-permute-start | bytes 196616 | tf_op jit(solution)/shard_map/ppermute | solution.py:505
  124.9 6.4 %shard_map.139.f_ref = bf16[4,64,512]{2,1,0:T(8,128)(2,1)S(1)} custom-call(bf16[4,84,16,128]{3,2,1,0:T(8,128)(2,1)S(1)} %shard_map.133.refs_8_.mine_ref, bf16[4,84,16,128]{3,2,1,0:T(8,128)(2,1)S(1)} %collective-permute-done.8.refs_9_.theirs_ref, f32[2,96,512]{2,1,0:T(8,128)S(1)} %shard_map.134.refs_10_.cf, ...), custom_call_target="tpu_custom_call" | custom-call | tf_op jit(solution)/shard_map/pallas_call | solution.py:507
  131.4 2.9 %shard_map.140 = (f32[60,1024]{1,0:T(8,128)}, f32[60,1024]{1,0:T(8,128)}, bf16[64,1024]{1,0:T(8,128)(2,1)}) custom-call(s32[6,16]{1,0:T(8,128)S(1)} %bitcast.25, f32[60,1024]{1,0:T(8,128)S(1)} %get-tuple-element.30.refs_12_.w_ref, bf16[2,64,512]{2,1,0:T(8,128)(2,1)S(1)} %get-tuple-element.32.fx_ref, bf16[4,64,512]{2,1,0:T(8,128)(2,1)S(1)} %shard_map.139.f_ref, ...), custom_call_target="tpu_custom_call" | custom-call | tf_op jit(solution)/shard_map/pallas_call | solution.py:510
  (36 shorter events, 0.1 us)
Async XLA Ops:
  0.6 0.9 copy-start.10
  1.8 8.4 %collective-permute-start = (bf16[42,16,128]{2,1,0:T(8,128)(2,1)S(1)}, bf16[42,16,128]{2,1,0:T(8,128)(2,1)S(1)}, u32[]{:S(2)}, u32[]{:S(2)}) collective-permute-start(bf16[42,16,128]{2,1,0:T(8,128)(2,1)S(1)} %shard_map.131), channel_id=1, source_target_pairs={{0,64},{8,72},{16,80},{24,88},{32,96},{40,104},{48,112},{56,120},{... | collective-permute-start | bytes 516104 | tf_op jit(solution)/shard_map/ppermute | solution.py:448
  11.6 4.6 %copy-start.13 = (s32[1,4]{1,0:T(1,128)S(1)}, s32[1,4]{1,0:T(1,128)}, u32[]{:S(2)}) copy-start(s32[1,4]{1,0:T(1,128)} %param.17) | copy-start | bytes 52
  11.6 22.6 %copy-start.11 = (s32[16,6]{0,1:T(8,128)S(1)}, s32[16,6]{0,1:T(8,128)}, u32[]{:S(2)}) copy-start(s32[16,6]{0,1:T(8,128)} %param.18) | copy-start | bytes 1156
  11.6 22.6 %all-to-all-start = ((bf16[4,2,42,16,128]{4,3,2,1,0:T(8,128)(2,1)}), bf16[4,2,42,16,128]{4,3,2,1,0:T(8,128)(2,1)S(1)}, u32[]{:S(2)}, u32[]{:S(2)}) async-start(bf16[4,2,42,16,128]{4,3,2,1,0:T(8,128)(2,1)} %broadcast_in_dim.9), calls=%async_computation | async-start | bytes 2752512 | tf_op jit(solution)/shard_map/all_to_all | solution.py:451
  36.4 39.3 %collective-permute-start.8 = (bf16[4,84,16,128]{3,2,1,0:T(8,128)(2,1)S(1)}, bf16[4,84,16,128]{3,2,1,0:T(8,128)(2,1)S(1)}, u32[]{:S(2)}, u32[]{:S(2)}) collective-permute-start(bf16[4,84,16,128]{3,2,1,0:T(8,128)(2,1)S(1)} %shard_map.133.refs_8_.mine_ref), channel_id=1, source_target_pairs={{0,8},{8,0},{16,24},{24,16},{32,40},{40,32},{48,56},{56,48},{64,72... | collective-permute-start | bytes 4128776 | tf_op jit(solution)/shard_map/ppermute | solution.py:465
  38.8 9.0 %collective-permute-start.4 = (bf16[128,1024]{1,0:T(8,128)(2,1)}, bf16[128,1024]{1,0:T(8,128)(2,1)S(1)}, u32[]{:S(2)}, u32[]{:S(2)}) collective-permute-start(bf16[128,1024]{1,0:T(8,128)(2,1)} %get-tuple-element.23.refs_0_), channel_id=1, source_target_pairs={{0,1},{1,0},{2,3},{3,2},{4,5},{5,4},{6,7},{7,6},{8,9},{9,8},{10,11... | collective-permute-start | bytes 786440 | tf_op jit(solution)/shard_map/ppermute | solution.py:404
  39.8 14.7 %collective-permute-start.3 = (bf16[128,1024]{1,0:T(8,128)(2,1)}, bf16[128,1024]{1,0:T(8,128)(2,1)S(1)}, u32[]{:S(2)}, u32[]{:S(2)}) collective-permute-start(bf16[128,1024]{1,0:T(8,128)(2,1)} %get-tuple-element.23.refs_0_), channel_id=1, source_target_pairs={{0,6},{1,7},{2,0},{3,1},{4,2},{5,3},{6,4},{7,5},{8,14},{9,15},{10,... | collective-permute-start | bytes 786440 | tf_op jit(solution)/shard_map/ppermute | solution.py:407
  42.6 12.9 %collective-permute-start.2 = (bf16[128,1024]{1,0:T(8,128)(2,1)}, bf16[128,1024]{1,0:T(8,128)(2,1)S(1)}, u32[]{:S(2)}, u32[]{:S(2)}) collective-permute-start(bf16[128,1024]{1,0:T(8,128)(2,1)} %get-tuple-element.23.refs_0_), channel_id=1, source_target_pairs={{0,4},{1,5},{2,6},{3,7},{4,0},{5,1},{6,2},{7,3},{8,12},{9,13},{10,... | collective-permute-start | bytes 786440 | tf_op jit(solution)/shard_map/ppermute | solution.py:406
  43.4 14.9 %collective-permute-start.1 = (bf16[128,1024]{1,0:T(8,128)(2,1)}, bf16[128,1024]{1,0:T(8,128)(2,1)}, u32[]{:S(2)}, u32[]{:S(2)}) collective-permute-start(bf16[128,1024]{1,0:T(8,128)(2,1)} %get-tuple-element.23.refs_0_), channel_id=1, source_target_pairs={{0,2},{1,3},{2,4},{3,5},{4,6},{5,7},{6,0},{7,1},{8,10},{9,11},{10,... | collective-permute-start | bytes 786440 | tf_op jit(solution)/shard_map/ppermute | solution.py:405
  47.8 16.0 %collective-permute-start.5 = (bf16[128,1024]{1,0:T(8,128)(2,1)S(1)}, bf16[128,1024]{1,0:T(8,128)(2,1)}, u32[]{:S(2)}, u32[]{:S(2)}) collective-permute-start(bf16[128,1024]{1,0:T(8,128)(2,1)S(1)} %collective-permute-done.4.refs_4_), channel_id=1, source_target_pairs={{0,2},{1,3},{2,4},{3,5},{4,6},{5,7},{6,0},{7,1},{8,10},{9,11},{10,... | collective-permute-start | bytes 786440 | tf_op jit(solution)/shard_map/ppermute | solution.py:414
  54.5 9.3 %collective-permute-start.7 = (bf16[128,1024]{1,0:T(8,128)(2,1)S(1)}, bf16[128,1024]{1,0:T(8,128)(2,1)}, u32[]{:S(2)}, u32[]{:S(2)}) collective-permute-start(bf16[128,1024]{1,0:T(8,128)(2,1)S(1)} %collective-permute-done.3.refs_3_), channel_id=1, source_target_pairs={{0,1},{1,0},{2,3},{3,2},{4,5},{5,4},{6,7},{7,6},{8,9},{9,8},{10,11... | collective-permute-start | bytes 786440 | tf_op jit(solution)/shard_map/ppermute | solution.py:416
  55.5 12.1 %collective-permute-start.6 = (bf16[128,1024]{1,0:T(8,128)(2,1)S(1)}, bf16[128,1024]{1,0:T(8,128)(2,1)}, u32[]{:S(2)}, u32[]{:S(2)}) collective-permute-start(bf16[128,1024]{1,0:T(8,128)(2,1)S(1)} %collective-permute-done.2.refs_2_), channel_id=1, source_target_pairs={{0,1},{1,0},{2,3},{3,2},{4,5},{5,4},{6,7},{7,6},{8,9},{9,8},{10,11... | collective-permute-start | bytes 786440 | tf_op jit(solution)/shard_map/ppermute | solution.py:415
  67.6 1.0 copy-start.2
  68.6 1.2 copy-start.6
  69.8 5.9 %copy-start.3 = (bf16[128,1024]{1,0:T(8,128)(2,1)S(1)}, bf16[128,1024]{1,0:T(8,128)(2,1)}, u32[]{:S(2)}) copy-start(bf16[128,1024]{1,0:T(8,128)(2,1)} %get-tuple-element.23.refs_0_) | copy-start | bytes 786436
  69.8 5.9 %copy-start.4 = (f32[60,1024]{1,0:T(8,128)S(1)}, f32[60,1024]{1,0:T(8,128)}, u32[]{:S(2)}) copy-start(f32[60,1024]{1,0:T(8,128)} %get-tuple-element.21.refs_12_.w_ref) | copy-start | bytes 737284
  69.8 5.9 %copy-start.5 = (bf16[2,512,128]{2,1,0:T(8,128)(2,1)S(1)}, bf16[2,512,128]{2,1,0:T(8,128)(2,1)}, u32[]{:S(2)}) copy-start(bf16[2,512,128]{2,1,0:T(8,128)(2,1)} %constant.117.clone.refs_13_) | copy-start | bytes 786436
  69.8 5.9 %copy-start.7 = (bf16[256,384]{1,0:T(8,128)(2,1)S(1)}, bf16[256,384]{1,0:T(8,128)(2,1)}, u32[]{:S(2)}) copy-start(bf16[256,384]{1,0:T(8,128)(2,1)} %constant.114.clone.refs_11_) | copy-start | bytes 589828
  82.3 11.9 %collective-permute-start.9 = (f32[64,256]{1,0:T(8,128)S(1)}, f32[64,256]{1,0:T(8,128)S(1)}, u32[]{:S(2)}, u32[]{:S(2)}) collective-permute-start(f32[64,256]{1,0:T(8,128)S(1)} %get-tuple-element.28), channel_id=1, source_target_pairs={{0,8},{8,16},{16,24},{24,32},{32,40},{40,48},{48,56},{56,64},{64,7... | collective-permute-start | bytes 196616 | tf_op jit(solution)/shard_map/ppermute | solution.py:506
  82.3 11.8 %collective-permute-start.10 = (f32[64,256]{1,0:T(8,128)S(1)}, f32[64,256]{1,0:T(8,128)S(1)}, u32[]{:S(2)}, u32[]{:S(2)}) collective-permute-start(f32[64,256]{1,0:T(8,128)S(1)} %get-tuple-element.29), channel_id=1, source_target_pairs={{0,120},{8,0},{16,8},{24,16},{32,24},{40,32},{48,40},{56,48},{64,5... | collective-permute-start | bytes 196616 | tf_op jit(solution)/shard_map/ppermute | solution.py:505
  87.7 6.5 %copy-start = (f32[60,1024]{1,0:T(8,128)S(1)}, f32[60,1024]{1,0:T(8,128)}, u32[]{:S(2)}) copy-start(f32[60,1024]{1,0:T(8,128)} %res_ref.5) | copy-start | bytes 737284
  87.7 6.5 %copy-start.1 = (f32[64,1024]{1,0:T(8,128)S(1)}, f32[64,1024]{1,0:T(8,128)}, u32[]{:S(2)}) copy-start(f32[64,1024]{1,0:T(8,128)} %inv_ref.5) | copy-start | bytes 786436
  87.7 6.5 %copy-start.8 = (bf16[2,384,128]{2,1,0:T(8,128)(2,1)S(1)}, bf16[2,384,128]{2,1,0:T(8,128)(2,1)}, u32[]{:S(2)}) copy-start(bf16[2,384,128]{2,1,0:T(8,128)(2,1)} %constant.115.clone.own_ref) | copy-start | bytes 589828
  87.7 6.5 %copy-start.9 = (bf16[256,128]{1,0:T(8,128)(2,1)S(1)}, bf16[256,128]{1,0:T(8,128)(2,1)}, u32[]{:S(2)}) copy-start(bf16[256,128]{1,0:T(8,128)(2,1)} %constant.116.clone.near_ref) | copy-start | bytes 196612
  87.7 6.5 %copy-start.12 = (f32[1,128]{1,0:T(1,128)S(1)}, f32[1,128]{1,0:T(1,128)}, u32[]{:S(2)}) copy-start(f32[1,128]{1,0:T(1,128)} %constant.118.clone.count_ref) | copy-start | bytes 1540
  96.9 5.8 %collective-permute-start.14 = (bf16[64,1024]{1,0:T(8,128)(2,1)S(1)}, bf16[64,1024]{1,0:T(8,128)(2,1)S(1)}, u32[]{:S(2)}, u32[]{:S(2)}) collective-permute-start(bf16[64,1024]{1,0:T(8,128)(2,1)S(1)} %get-tuple-element.31.refs_0_), channel_id=1, source_target_pairs={{0,1},{1,0},{2,3},{3,2},{4,5},{5,4},{6,7},{7,6},{8,9},{9,8},{10,11... | collective-permute-start | bytes 393224 | tf_op jit(solution)/shard_map/ppermute | solution.py:404
  98.0 7.8 %collective-permute-start.13 = (bf16[64,1024]{1,0:T(8,128)(2,1)S(1)}, bf16[64,1024]{1,0:T(8,128)(2,1)S(1)}, u32[]{:S(2)}, u32[]{:S(2)}) collective-permute-start(bf16[64,1024]{1,0:T(8,128)(2,1)S(1)} %get-tuple-element.31.refs_0_), channel_id=1, source_target_pairs={{0,6},{1,7},{2,0},{3,1},{4,2},{5,3},{6,4},{7,5},{8,14},{9,15},{10,... | collective-permute-start | bytes 393224 | tf_op jit(solution)/shard_map/ppermute | solution.py:407
  101.9 6.6 %collective-permute-start.12 = (bf16[64,1024]{1,0:T(8,128)(2,1)S(1)}, bf16[64,1024]{1,0:T(8,128)(2,1)S(1)}, u32[]{:S(2)}, u32[]{:S(2)}) collective-permute-start(bf16[64,1024]{1,0:T(8,128)(2,1)S(1)} %get-tuple-element.31.refs_0_), channel_id=1, source_target_pairs={{0,4},{1,5},{2,6},{3,7},{4,0},{5,1},{6,2},{7,3},{8,12},{9,13},{10,... | collective-permute-start | bytes 393224 | tf_op jit(solution)/shard_map/ppermute | solution.py:406
  101.9 7.6 %collective-permute-start.11 = (bf16[64,1024]{1,0:T(8,128)(2,1)S(1)}, bf16[64,1024]{1,0:T(8,128)(2,1)S(1)}, u32[]{:S(2)}, u32[]{:S(2)}) collective-permute-start(bf16[64,1024]{1,0:T(8,128)(2,1)S(1)} %get-tuple-element.31.refs_0_), channel_id=1, source_target_pairs={{0,2},{1,3},{2,4},{3,5},{4,6},{5,7},{6,0},{7,1},{8,10},{9,11},{10,... | collective-permute-start | bytes 393224 | tf_op jit(solution)/shard_map/ppermute | solution.py:405
  102.7 8.1 %collective-permute-start.15 = (bf16[64,1024]{1,0:T(8,128)(2,1)S(1)}, bf16[64,1024]{1,0:T(8,128)(2,1)S(1)}, u32[]{:S(2)}, u32[]{:S(2)}) collective-permute-start(bf16[64,1024]{1,0:T(8,128)(2,1)S(1)} %collective-permute-done.14.refs_4_), channel_id=1, source_target_pairs={{0,2},{1,3},{2,4},{3,5},{4,6},{5,7},{6,0},{7,1},{8,10},{9,11},{10,... | collective-permute-start | bytes 393224 | tf_op jit(solution)/shard_map/ppermute | solution.py:414
  105.8 5.1 %collective-permute-start.17 = (bf16[64,1024]{1,0:T(8,128)(2,1)S(1)}, bf16[64,1024]{1,0:T(8,128)(2,1)S(1)}, u32[]{:S(2)}, u32[]{:S(2)}) collective-permute-start(bf16[64,1024]{1,0:T(8,128)(2,1)S(1)} %collective-permute-done.13.refs_3_), channel_id=1, source_target_pairs={{0,1},{1,0},{2,3},{3,2},{4,5},{5,4},{6,7},{7,6},{8,9},{9,8},{10,11... | collective-permute-start | bytes 393224 | tf_op jit(solution)/shard_map/ppermute | solution.py:416
  108.4 5.0 %collective-permute-start.16 = (bf16[64,1024]{1,0:T(8,128)(2,1)S(1)}, bf16[64,1024]{1,0:T(8,128)(2,1)S(1)}, u32[]{:S(2)}, u32[]{:S(2)}) collective-permute-start(bf16[64,1024]{1,0:T(8,128)(2,1)S(1)} %collective-permute-done.12.refs_2_), channel_id=1, source_target_pairs={{0,1},{1,0},{2,3},{3,2},{4,5},{5,4},{6,7},{7,6},{8,9},{9,8},{10,11... | collective-permute-start | bytes 393224 | tf_op jit(solution)/shard_map/ppermute | solution.py:415
  119.5 11.9 %collective-permute-start.18 = (f32[64,256]{1,0:T(8,128)S(1)}, f32[64,256]{1,0:T(8,128)S(1)}, u32[]{:S(2)}, u32[]{:S(2)}) collective-permute-start(f32[64,256]{1,0:T(8,128)S(1)} %get-tuple-element.34), channel_id=1, source_target_pairs={{0,8},{8,16},{16,24},{24,32},{32,40},{40,48},{48,56},{56,64},{64,7... | collective-permute-start | bytes 196616 | tf_op jit(solution)/shard_map/ppermute | solution.py:506
  119.6 11.8 %collective-permute-start.19 = (f32[64,256]{1,0:T(8,128)S(1)}, f32[64,256]{1,0:T(8,128)S(1)}, u32[]{:S(2)}, u32[]{:S(2)}) collective-permute-start(f32[64,256]{1,0:T(8,128)S(1)} %get-tuple-element.35), channel_id=1, source_target_pairs={{0,120},{8,0},{16,8},{24,16},{32,24},{40,32},{48,40},{56,48},{64,5... | collective-permute-start | bytes 196616 | tf_op jit(solution)/shard_map/ppermute | solution.py:505

commit v3 on v2

--- a/solution.py
+++ b/solution.py
@@ -169,7 +169,8 @@
     side = side_ref[0]
     place_row = lax.broadcasted_iota(jnp.int32, (128, 128), 0)
     place_column = lax.broadcasted_iota(jnp.int32, (128, 128), 1)
-    eye = jnp.where(place_row == place_column, 1.0, 0.0).astype(BF)
+    half, group, inner = (place_row // 4) % 2, place_row // 8, place_row % 4
+    order = jnp.where(place_column == 64 * half + 4 * group + inner, 1.0, 0.0).astype(BF)
 
     def step(twin, carry):
         rows = []
@@ -178,18 +179,15 @@
             rows.append(held[place % 4, zone, pl.ds(2 * twin, 2)])
         both = jnp.concatenate([row[pair] for pair in range(2) for row in rows], axis=0)
         turned = lax.dot_general(
-            eye, both, (((1,), (1,)), ((), ())), preferred_element_type=F32
-        ).astype(BF)
-        for pair in range(2):
-            for half in range(2):
-                for tile in range(4):
-                    first = 64 * half + 16 * tile
-                    tt_ref[tile, 4 * twin + 2 * pair + half] = turned[
-                        first : first + 16, 128 * pair : 128 * pair + 128
-                    ]
+            order, both, (((1,), (1,)), ((), ())), preferred_element_type=F32
+        )
+        for group in range(15):
+            rows = slice(8 * group, 8 * group + 8)
+            pair = jnp.concatenate([turned[rows, 0:128], turned[rows, 128:256]], axis=0)
+            tt_ref[group, twin] = pair.astype(BF)
         return carry
 
-    lax.fori_loop(0, PAIRS // 2, step, 0, unroll=3)
+    lax.fori_loop(0, PAIRS // 2, step, 0, unroll=7)
 
 
 def coefficient_body(spot_ref, *refs):
@@ -209,12 +207,17 @@
         copy.wait()
     for block in range(8):
         joined[60 * block : 60 * block + 60, :] = low[block].astype(F32)[0:60]
+    upper = lax.broadcasted_iota(jnp.int32, (8, 256), 0) < 4
     for quarter in range(4):
         state = joined[:, 256 * quarter : 256 * quarter + 256].astype(BF)
         growth = jnp.exp(GROWTH * dot(basis[...], state))
         high, rest = split(growth)
         terms = (dot(lead, high) + dot(lead, rest)) * (1.0 / S)
-        c_ref[quarter // 2, :, 256 * (quarter % 2) : 256 * (quarter % 2) + 256] = terms.astype(BF).astype(F32)
+        terms = terms.astype(BF).astype(F32)
+        for pair in range(PAIRS):
+            c_ref[quarter // 2, pair, :, 256 * (quarter % 2) : 256 * (quarter % 2) + 256] = jnp.where(
+                upper, terms[2 * pair : 2 * pair + 1], terms[2 * pair + 1 : 2 * pair + 2]
+            )
 
 
 def invert(field, inv_ref, out_ref, base, weight):
@@ -253,24 +256,30 @@
     pad_modes(value, padded, wp_ref)
 
 
-def weighted(mine_ref, theirs_ref, grad, cf, half, out_ref, tile):
-    for part in range(4):
+def weighted(mine_ref, theirs_ref, grad, cf, half, out_ref, tile, whole):
+    for block in range(5):
+        rows = slice(3 * block, 3 * block + 3)
         left = jnp.concatenate(
-            [mine_ref[part].reshape(K * 16, 128), theirs_ref[part].reshape(K * 16, 128)], axis=1
+            [mine_ref[rows].reshape(24 * PAIRS, 128), theirs_ref[rows].reshape(24 * PAIRS, 128)], axis=1
         )
         terms = dot(left, grad)
-        total = None
-        for k in range(K):
-            term = cf[half, k : k + 1, :] * terms[16 * k : 16 * k + 16]
-            total = term if total is None else total + term
-        out_ref[tile, 16 * part : 16 * part + 16, :] = total.astype(BF)
+        for inner in range(3):
+            total = None
+            for pair in range(PAIRS):
+                first = 8 * (PAIRS * inner + pair)
+                term = cf[half, pair] * terms[first : first + 8]
+                total = term if total is None else total + term
+            group = 3 * block + inner
+            whole[4 * group : 4 * group + 4, :] = total[0:4] + total[4:8]
+    out_ref[tile] = whole[...].astype(BF)
 
 
 def along_body(slot_ref, core_ref, *refs):
     blocks = refs[0:8]
     mine_ref, theirs_ref, cf, table_src, w_src, trace_src = refs[8:14]
     f_ref, toward_ref, onward_ref, grads_ref = refs[14:18]
-    picked, first_grads, sem, table_ref, w_ref, trace_ref, late = refs[18:25]
+    picked, first_grads, sem, table_ref, w_ref, trace_ref, late, whole = refs[18:26]
+    whole[60:64, :] = jnp.zeros((4, 512), F32)
     copies = fetch((table_src, w_src, trace_src), (table_ref, w_ref, trace_ref), late)
     for stored in range(4):
         for index in range(8):
@@ -300,7 +309,7 @@
 
     def step(half, carry):
         grad = first_grads[half].reshape(256, 512)
-        weighted(mine_ref, theirs_ref, grad, cf, half, f_ref, half)
+        weighted(mine_ref, theirs_ref, grad, cf, half, f_ref, half, whole)
         return carry
 
     lax.fori_loop(0, 2, step, 0)
@@ -320,10 +329,12 @@
             out_ref[:, 128 * half : 128 * half + 128] = dot(high, table) + dot(low, table)
 
 
-def across_body(mine_ref, theirs_ref, cf, grads_ref, f_ref):
+def across_body(mine_ref, theirs_ref, cf, grads_ref, f_ref, whole):
+    whole[60:64, :] = jnp.zeros((4, 512), F32)
+
     def step(tile, carry):
         grad = grads_ref[tile].reshape(256, 512)
-        weighted(mine_ref, theirs_ref, grad, cf, lax.rem(tile, 2), f_ref, tile)
+        weighted(mine_ref, theirs_ref, grad, cf, lax.rem(tile, 2), f_ref, tile, whole)
         return carry
 
     lax.fori_loop(0, 4, step, 0)
@@ -459,13 +470,13 @@
     pieces = over_mode(padded)
 
     held, slots, spots, ids = lax.optimization_barrier((held, slots, spots, neighbour_ids.T))
-    (mine,) = call(turn_body, (shaped((4, K, 16, 128), BF),), (SMEM,) * 2 + (VMEM,), ())(
+    (mine,) = call(turn_body, (shaped((15, PAIRS // 2, 16, 128), BF),), (SMEM,) * 2 + (VMEM,), ())(
         side, ids, held
     )
     theirs = lax.ppermute(mine, "elem", pairs_of(16, lambda i: i ^ 1))
     (coeffs,) = call(
         coefficient_body,
-        (shaped((2, 96, 512), F32),),
+        (shaped((2, PAIRS, 8, 512), F32),),
         (SMEM,) + (ANY,) * 9,
         (
             pltpu.VMEM((8, ROWS, NODES), BF),
@@ -500,11 +511,12 @@
                 pltpu.VMEM((MB, NODES), F32),
                 pltpu.VMEM((2, 512, 128), BF),
                 pltpu.SemaphoreType.DMA((3,)),
+                pltpu.VMEM((ROWS, 512), F32),
             ),
         )(slots, core, *pieces, mine, theirs, coeffs, gradients_of, correction, traces)
         after = lax.ppermute(toward, "elem", pairs_of(16, lambda i: (i + 15) % 16))
         before = lax.ppermute(onward, "elem", pairs_of(16, lambda i: (i + 1) % 16))
-        (across,) = call(across_body, (shaped((4, ROWS, 512), BF),), (VMEM,) * 4, ())(
+        (across,) = call(across_body, (shaped((4, ROWS, 512), BF),), (VMEM,) * 4, (pltpu.VMEM((ROWS, 512), F32),))(
             mine, theirs, coeffs, grads
         )
         remainder, correction, padded = call(

time: 135 us -> 133 us (0.985)
  no operation moved by 1% of the time
where the time goes in v3:
time: 133 us
  waiting for transfers between devices  48.4 us (36%)
  Pallas kernels  40.4 us (30%)
  starting transfers between devices  38.8 us (29%)
  local copies, waits for them, and re-layouts  4.4 us (3%)
    all_to_all x1, waiting for transfers between devices, per_device(): held = lax.all_to_all(sent, 'elem', 0, 0, axis_index_groups=groups)  18 us
    pallas_call x2, Pallas kernels, per_device(): call(across_body, (shaped((4, ROWS, 512), BF),), (VMEM,) * 4, (pltpu.VMEM...  12.4 us
    pallas_call x2, Pallas kernels, per_device(): call(along_body, (shaped((2, ROWS, 512), BF), shaped((ROWS, 256), F32), s...  12.3 us
    ppermute x2, starting transfers between devices, per_device(): after = lax.ppermute(toward, 'elem', pairs_of(16, lambda i: (i + 15) % 16))  10.7 us
    ppermute x2, waiting for transfers between devices, over_mode(): lax.ppermute(other, 'mode', along(1))  6.93 us
    ppermute x2, starting transfers between devices, over_mode(): three = lax.ppermute(block, 'mode', along(3))  6.63 us
    ppermute x2, waiting for transfers between devices, over_mode(): lax.ppermute(two, 'mode', flip)  6.36 us
    pallas_call x1, Pallas kernels, per_device(): call(coefficient_body, (shaped((2, PAIRS, 8, 512), F32),), (SMEM,) + (ANY...  5.92 us
  transfers between devices with their start and end apart: 21, of which 12 were waited for; matrix products, arithmetic and copies ran while one was open for 0% of the time, Pallas kernels for 16%

profile of v3, /device:TPU:0, one launch (start us, length us, event | category | flops | bytes accessed | tf_op | source)
XLA Modules:
  0.0 133.0 jit_solution(288805562364866095)
XLA Ops:
  0.6 0.9 copy-done.10
  1.5 0.3 shard_map.131
  1.8 4.1 %collective-permute-start = (bf16[42,16,128]{2,1,0:T(8,128)(2,1)S(1)}, bf16[42,16,128]{2,1,0:T(8,128)(2,1)S(1)}, u32[]{:S(2)}, u32[]{:S(2)}) collective-permute-start(bf16[42,16,128]{2,1,0:T(8,128)(2,1)S(1)} %shard_map.131), channel_id=1, source_target_pairs={{0,64},{8,72},{16,80},{24,88},{32,96},{40,104},{48,112},{56,120},{... | collective-permute-start | bytes 516104 | tf_op jit(solution)/shard_map/ppermute | solution.py:459
  5.9 4.4 %collective-permute-done = bf16[42,16,128]{2,1,0:T(8,128)(2,1)S(1)} collective-permute-done((bf16[42,16,128]{2,1,0:T(8,128)(2,1)S(1)}, bf16[42,16,128]{2,1,0:T(8,128)(2,1)S(1)}, u32[]{:S(2)}, u32[]{:S(2)}) %collective-permute-start) | collective-permute-done | bytes 172064 | tf_op jit(solution)/shard_map/ppermute | solution.py:459
  10.3 1.3 broadcast_in_dim.9
  11.6 4.6 %all-to-all-start = ((bf16[4,2,42,16,128]{4,3,2,1,0:T(8,128)(2,1)}), bf16[4,2,42,16,128]{4,3,2,1,0:T(8,128)(2,1)S(1)}, u32[]{:S(2)}, u32[]{:S(2)}) async-start(bf16[4,2,42,16,128]{4,3,2,1,0:T(8,128)(2,1)} %broadcast_in_dim.9), calls=%async_computation | async-start | bytes 2752512 | tf_op jit(solution)/shard_map/all_to_all | solution.py:462
  16.2 18.0 %all-to-all-done.held = bf16[4,2,42,16,128]{4,3,2,1,0:T(8,128)(2,1)S(1)} async-done(((bf16[4,2,42,16,128]{4,3,2,1,0:T(8,128)(2,1)}), bf16[4,2,42,16,128]{4,3,2,1,0:T(8,128)(2,1)S(1)}, u32[]{:S(2)}, u32[]{:S(2)}) %all-to-all-start) | async-done | bytes 1376288 | tf_op jit(solution)/shard_map/all_to_all | solution.py:462
  34.2 1.5 %shard_map.133.refs_8_.mine_ref = bf16[15,21,16,128]{3,2,1,0:T(8,128)(2,1)S(1)} custom-call(s32[1]{0:T(128)} %bitcast.6.side_ref, s32[6,16]{1,0:T(8,128)S(1)} %bitcast.23, bf16[4,2,42,16,128]{4,3,2,1,0:T(8,128)(2,1)S(1)} %all-to-all-done.held), custom_call_target="tpu_custom_call" | custom-call | tf_op jit(solution)/shard_map/pallas_call | solution.py:473
  35.7 0.1 collective-permute-start.8
  35.8 2.3 %shard_map.132 = (f32[60,1024]{1,0:T(8,128)}, bf16[128,1024]{1,0:T(8,128)(2,1)}) custom-call(f32[60,1024]{1,0:T(8,128)} %res_ref.5, f32[64,1024]{1,0:T(8,128)} %inv_ref.5, f32[60,1024]{1,0:T(8,128)} %state_ref.1), custom_call_target="tpu_custom_call" | custom-call | tf_op jit(solution)/shard_map/pallas_call | solution.py:463
  38.1 1.1 collective-permute-start.4
  39.2 2.8 %collective-permute-start.3 = (bf16[128,1024]{1,0:T(8,128)(2,1)}, bf16[128,1024]{1,0:T(8,128)(2,1)S(1)}, u32[]{:S(2)}, u32[]{:S(2)}) collective-permute-start(bf16[128,1024]{1,0:T(8,128)(2,1)} %get-tuple-element.23.refs_0_), channel_id=1, source_target_pairs={{0,6},{1,7},{2,0},{3,1},{4,2},{5,3},{6,4},{7,5},{8,14},{9,15},{10,... | collective-permute-start | bytes 786440 | tf_op jit(solution)/shard_map/ppermute | solution.py:418
  42.0 0.8 collective-permute-start.2
  42.8 0.9 collective-permute-start.1
  43.6 3.5 %collective-permute-done.4.refs_4_ = bf16[128,1024]{1,0:T(8,128)(2,1)S(1)} collective-permute-done((bf16[128,1024]{1,0:T(8,128)(2,1)}, bf16[128,1024]{1,0:T(8,128)(2,1)S(1)}, u32[]{:S(2)}, u32[]{:S(2)}) %collective-permute-start.4) | collective-permute-done | bytes 262176 | tf_op jit(solution)/shard_map/ppermute | solution.py:415
  47.1 1.5 %collective-permute-start.5 = (bf16[128,1024]{1,0:T(8,128)(2,1)S(1)}, bf16[128,1024]{1,0:T(8,128)(2,1)}, u32[]{:S(2)}, u32[]{:S(2)}) collective-permute-start(bf16[128,1024]{1,0:T(8,128)(2,1)S(1)} %collective-permute-done.4.refs_4_), channel_id=1, source_target_pairs={{0,2},{1,3},{2,4},{3,5},{4,6},{5,7},{6,0},{7,1},{8,10},{9,11},{10,... | collective-permute-start | bytes 786440 | tf_op jit(solution)/shard_map/ppermute | solution.py:425
  48.6 5.3 %collective-permute-done.3.refs_3_ = bf16[128,1024]{1,0:T(8,128)(2,1)S(1)} collective-permute-done((bf16[128,1024]{1,0:T(8,128)(2,1)}, bf16[128,1024]{1,0:T(8,128)(2,1)S(1)}, u32[]{:S(2)}, u32[]{:S(2)}) %collective-permute-start.3) | collective-permute-done | bytes 262176 | tf_op jit(solution)/shard_map/ppermute | solution.py:418
  53.9 1.0 collective-permute-start.7
  54.9 1.0 collective-permute-start.6
  55.9 1.7 %collective-permute-done.1.refs_1_ = bf16[128,1024]{1,0:T(8,128)(2,1)} collective-permute-done((bf16[128,1024]{1,0:T(8,128)(2,1)}, bf16[128,1024]{1,0:T(8,128)(2,1)}, u32[]{:S(2)}, u32[]{:S(2)}) %collective-permute-start.1) | collective-permute-done | bytes 262176 | tf_op jit(solution)/shard_map/ppermute | solution.py:416
  57.6 5.5 %collective-permute-done.5.refs_5_ = bf16[128,1024]{1,0:T(8,128)(2,1)} collective-permute-done((bf16[128,1024]{1,0:T(8,128)(2,1)S(1)}, bf16[128,1024]{1,0:T(8,128)(2,1)}, u32[]{:S(2)}, u32[]{:S(2)}) %collective-permute-start.5) | collective-permute-done | bytes 262176 | tf_op jit(solution)/shard_map/ppermute | solution.py:425
  63.2 3.8 %collective-permute-done.6.refs_6_ = bf16[128,1024]{1,0:T(8,128)(2,1)} collective-permute-done((bf16[128,1024]{1,0:T(8,128)(2,1)S(1)}, bf16[128,1024]{1,0:T(8,128)(2,1)}, u32[]{:S(2)}, u32[]{:S(2)}) %collective-permute-start.6) | collective-permute-done | bytes 262176 | tf_op jit(solution)/shard_map/ppermute | solution.py:426
  67.0 0.9 copy-done.3
  67.9 1.2 copy-done.6
  69.2 5.9 %shard_map.134.refs_10_.cf = f32[2,42,8,512]{3,2,1,0:T(8,128)S(1)} custom-call(s32[8]{0:T(128)S(1)} %fusion.5.spot_ref, bf16[128,1024]{1,0:T(8,128)(2,1)S(1)} %copy-done.3, bf16[128,1024]{1,0:T(8,128)(2,1)} %collective-permute-done.1.refs_1_, bf16[128,1024]{1,0:T(8,128)(2,1)S(1)} %collective-permute-done.2.refs_2_, ...), custom_call_target="tpu_custom_call" | custom-call | tf_op jit(solution)/shard_map/pallas_call | solution.py:477
  75.1 0.0 collective-permute-done.8.refs_9_.theirs_ref
  75.1 6.4 %shard_map.135 = (bf16[2,64,512]{2,1,0:T(8,128)(2,1)S(1)}, f32[64,256]{1,0:T(8,128)S(1)}, f32[64,256]{1,0:T(8,128)S(1)}, bf16[4,16,16,512]{3,2,1,0:T(8,128)(2,1)S(1)}) custom-call(s32[4]{0:T(128)S(1)} %fusion.slot_ref, s32[1]{0:T(128)} %bitcast.5.core_ref, bf16[128,1024]{1,0:T(8,128)(2,1)S(1)} %copy-done.4, ...), custom_call_target="tpu_custom_call" | custom-call | tf_op jit(solution)/shard_map/pallas_call | solution.py:497
  81.5 0.1 collective-permute-start.9
  81.6 5.3 %collective-permute-start.10 = (f32[64,256]{1,0:T(8,128)S(1)}, f32[64,256]{1,0:T(8,128)S(1)}, u32[]{:S(2)}, u32[]{:S(2)}) collective-permute-start(f32[64,256]{1,0:T(8,128)S(1)} %get-tuple-element.29), channel_id=1, source_target_pairs={{0,120},{8,0},{16,8},{24,16},{32,24},{40,32},{48,40},{56,48},{64,5... | collective-permute-start | bytes 196616 | tf_op jit(solution)/shard_map/ppermute | solution.py:517
  87.0 0.0 copy-start.12
  87.0 6.1 %shard_map.136.f_ref = bf16[4,64,512]{2,1,0:T(8,128)(2,1)S(1)} custom-call(bf16[15,21,16,128]{3,2,1,0:T(8,128)(2,1)S(1)} %shard_map.133.refs_8_.mine_ref, bf16[15,21,16,128]{3,2,1,0:T(8,128)(2,1)S(1)} %collective-permute-done.8.refs_9_.theirs_ref, f32[2,42,8,512]{3,2,1,0:T(8,128)S(1)} %shard_map.134.refs_10_.cf, ...), custom_call_target="tpu_custom_call" | custom-call | tf_op jit(solution)/shard_map/pallas_call | solution.py:519
  93.2 2.7 %shard_map.137 = (f32[60,1024]{1,0:T(8,128)}, f32[60,1024]{1,0:T(8,128)S(1)}, bf16[64,1024]{1,0:T(8,128)(2,1)S(1)}) custom-call(s32[6,16]{1,0:T(8,128)S(1)} %bitcast.24, f32[60,1024]{1,0:T(8,128)S(1)} %copy-done.5, bf16[2,64,512]{2,1,0:T(8,128)(2,1)S(1)} %get-tuple-element.26.fx_ref, bf16[4,64,512]{2,1,0:T(8,128)(2,1)S(1)} %shard_map.136.f_ref, ...), custom_call_target="tpu_custom_call" | custom-call | tf_op jit(solution)/shard_map/pallas_call | solution.py:522
  95.9 1.1 collective-permute-start.14
  97.0 3.9 %collective-permute-start.13 = (bf16[64,1024]{1,0:T(8,128)(2,1)S(1)}, bf16[64,1024]{1,0:T(8,128)(2,1)S(1)}, u32[]{:S(2)}, u32[]{:S(2)}) collective-permute-start(bf16[64,1024]{1,0:T(8,128)(2,1)S(1)} %get-tuple-element.31.refs_0_), channel_id=1, source_target_pairs={{0,6},{1,7},{2,0},{3,1},{4,2},{5,3},{6,4},{7,5},{8,14},{9,15},{10,... | collective-permute-start | bytes 393224 | tf_op jit(solution)/shard_map/ppermute | solution.py:418
  100.8 0.9 collective-permute-start.11
  101.7 2.6 %collective-permute-start.15 = (bf16[64,1024]{1,0:T(8,128)(2,1)S(1)}, bf16[64,1024]{1,0:T(8,128)(2,1)S(1)}, u32[]{:S(2)}, u32[]{:S(2)}) collective-permute-start(bf16[64,1024]{1,0:T(8,128)(2,1)S(1)} %collective-permute-done.14.refs_4_), channel_id=1, source_target_pairs={{0,2},{1,3},{2,4},{3,5},{4,6},{5,7},{6,0},{7,1},{8,10},{9,11},{10,... | collective-permute-start | bytes 393224 | tf_op jit(solution)/shard_map/ppermute | solution.py:425
  104.3 0.4 collective-permute-done.13.refs_3_
  104.7 0.9 collective-permute-start.17
  105.6 1.7 %collective-permute-done.12.refs_2_ = bf16[64,1024]{1,0:T(8,128)(2,1)S(1)} collective-permute-done((bf16[64,1024]{1,0:T(8,128)(2,1)S(1)}, bf16[64,1024]{1,0:T(8,128)(2,1)S(1)}, u32[]{:S(2)}, u32[]{:S(2)}) %collective-permute-start.12) | collective-permute-done | bytes 131104 | tf_op jit(solution)/shard_map/ppermute | solution.py:417
  107.4 0.9 collective-permute-start.16
  108.3 0.1 collective-permute-done.11.refs_1_
  108.4 1.4 %collective-permute-done.15.refs_5_ = bf16[64,1024]{1,0:T(8,128)(2,1)S(1)} collective-permute-done((bf16[64,1024]{1,0:T(8,128)(2,1)S(1)}, bf16[64,1024]{1,0:T(8,128)(2,1)S(1)}, u32[]{:S(2)}, u32[]{:S(2)}) %collective-permute-start.15) | collective-permute-done | bytes 131104 | tf_op jit(solution)/shard_map/ppermute | solution.py:425
  109.8 2.5 %collective-permute-done.16.refs_6_ = bf16[64,1024]{1,0:T(8,128)(2,1)S(1)} collective-permute-done((bf16[64,1024]{1,0:T(8,128)(2,1)S(1)}, bf16[64,1024]{1,0:T(8,128)(2,1)S(1)}, u32[]{:S(2)}, u32[]{:S(2)}) %collective-permute-start.16) | collective-permute-done | bytes 131104 | tf_op jit(solution)/shard_map/ppermute | solution.py:426
  112.4 5.9 %shard_map.138 = (bf16[2,64,512]{2,1,0:T(8,128)(2,1)S(1)}, f32[64,256]{1,0:T(8,128)S(1)}, f32[64,256]{1,0:T(8,128)S(1)}, bf16[4,16,16,512]{3,2,1,0:T(8,128)(2,1)S(1)}) custom-call(s32[4]{0:T(128)S(1)} %fusion.slot_ref, s32[1]{0:T(128)} %bitcast.5.core_ref, bf16[64,1024]{1,0:T(8,128)(2,1)S(1)} %get-tuple-element.31.refs_0_, ...), custom_call_target="tpu_custom_call" | custom-call | tf_op jit(solution)/shard_map/pallas_call | solution.py:497
  118.3 0.1 collective-permute-start.18
  118.4 5.3 %collective-permute-start.19 = (f32[64,256]{1,0:T(8,128)S(1)}, f32[64,256]{1,0:T(8,128)S(1)}, u32[]{:S(2)}, u32[]{:S(2)}) collective-permute-start(f32[64,256]{1,0:T(8,128)S(1)} %get-tuple-element.35), channel_id=1, source_target_pairs={{0,120},{8,0},{16,8},{24,16},{32,24},{40,32},{48,40},{56,48},{64,5... | collective-permute-start | bytes 196616 | tf_op jit(solution)/shard_map/ppermute | solution.py:517
  123.7 6.3 %shard_map.139.f_ref = bf16[4,64,512]{2,1,0:T(8,128)(2,1)S(1)} custom-call(bf16[15,21,16,128]{3,2,1,0:T(8,128)(2,1)S(1)} %shard_map.133.refs_8_.mine_ref, bf16[15,21,16,128]{3,2,1,0:T(8,128)(2,1)S(1)} %collective-permute-done.8.refs_9_.theirs_ref, f32[2,42,8,512]{3,2,1,0:T(8,128)S(1)} %shard_map.134.refs_10_.cf, ...), custom_call_target="tpu_custom_call" | custom-call | tf_op jit(solution)/shard_map/pallas_call | solution.py:519
  130.1 2.9 %shard_map.140 = (f32[60,1024]{1,0:T(8,128)}, f32[60,1024]{1,0:T(8,128)}, bf16[64,1024]{1,0:T(8,128)(2,1)}) custom-call(s32[6,16]{1,0:T(8,128)S(1)} %bitcast.25, f32[60,1024]{1,0:T(8,128)S(1)} %get-tuple-element.30.refs_12_.w_ref, bf16[2,64,512]{2,1,0:T(8,128)(2,1)S(1)} %get-tuple-element.32.fx_ref, bf16[4,64,512]{2,1,0:T(8,128)(2,1)S(1)} %shard_map.139.f_ref, ...), custom_call_target="tpu_custom_call" | custom-call | tf_op jit(solution)/shard_map/pallas_call | solution.py:522
  (36 shorter events, 0.1 us)
Async XLA Ops:
  0.6 0.9 copy-start.10
  1.8 8.4 %collective-permute-start = (bf16[42,16,128]{2,1,0:T(8,128)(2,1)S(1)}, bf16[42,16,128]{2,1,0:T(8,128)(2,1)S(1)}, u32[]{:S(2)}, u32[]{:S(2)}) collective-permute-start(bf16[42,16,128]{2,1,0:T(8,128)(2,1)S(1)} %shard_map.131), channel_id=1, source_target_pairs={{0,64},{8,72},{16,80},{24,88},{32,96},{40,104},{48,112},{56,120},{... | collective-permute-start | bytes 516104 | tf_op jit(solution)/shard_map/ppermute | solution.py:459
  11.6 4.6 %copy-start.13 = (s32[1,4]{1,0:T(1,128)S(1)}, s32[1,4]{1,0:T(1,128)}, u32[]{:S(2)}) copy-start(s32[1,4]{1,0:T(1,128)} %param.17) | copy-start | bytes 52
  11.6 22.6 %copy-start.11 = (s32[16,6]{0,1:T(8,128)S(1)}, s32[16,6]{0,1:T(8,128)}, u32[]{:S(2)}) copy-start(s32[16,6]{0,1:T(8,128)} %param.18) | copy-start | bytes 1156
  11.6 22.6 %all-to-all-start = ((bf16[4,2,42,16,128]{4,3,2,1,0:T(8,128)(2,1)}), bf16[4,2,42,16,128]{4,3,2,1,0:T(8,128)(2,1)S(1)}, u32[]{:S(2)}, u32[]{:S(2)}) async-start(bf16[4,2,42,16,128]{4,3,2,1,0:T(8,128)(2,1)} %broadcast_in_dim.9), calls=%async_computation | async-start | bytes 2752512 | tf_op jit(solution)/shard_map/all_to_all | solution.py:462
  35.7 39.4 %collective-permute-start.8 = (bf16[15,21,16,128]{3,2,1,0:T(8,128)(2,1)S(1)}, bf16[15,21,16,128]{3,2,1,0:T(8,128)(2,1)S(1)}, u32[]{:S(2)}, u32[]{:S(2)}) collective-permute-start(bf16[15,21,16,128]{3,2,1,0:T(8,128)(2,1)S(1)} %shard_map.133.refs_8_.mine_ref), channel_id=1, source_target_pairs={{0,8},{8,0},{16,24},{24,16},{32,40},{40,32},{48,56},{56,48},{64,72... | collective-permute-start | bytes 3870728 | tf_op jit(solution)/shard_map/ppermute | solution.py:476
  38.1 9.0 %collective-permute-start.4 = (bf16[128,1024]{1,0:T(8,128)(2,1)}, bf16[128,1024]{1,0:T(8,128)(2,1)S(1)}, u32[]{:S(2)}, u32[]{:S(2)}) collective-permute-start(bf16[128,1024]{1,0:T(8,128)(2,1)} %get-tuple-element.23.refs_0_), channel_id=1, source_target_pairs={{0,1},{1,0},{2,3},{3,2},{4,5},{5,4},{6,7},{7,6},{8,9},{9,8},{10,11... | collective-permute-start | bytes 786440 | tf_op jit(solution)/shard_map/ppermute | solution.py:415
  39.2 14.7 %collective-permute-start.3 = (bf16[128,1024]{1,0:T(8,128)(2,1)}, bf16[128,1024]{1,0:T(8,128)(2,1)S(1)}, u32[]{:S(2)}, u32[]{:S(2)}) collective-permute-start(bf16[128,1024]{1,0:T(8,128)(2,1)} %get-tuple-element.23.refs_0_), channel_id=1, source_target_pairs={{0,6},{1,7},{2,0},{3,1},{4,2},{5,3},{6,4},{7,5},{8,14},{9,15},{10,... | collective-permute-start | bytes 786440 | tf_op jit(solution)/shard_map/ppermute | solution.py:418
  42.0 12.9 %collective-permute-start.2 = (bf16[128,1024]{1,0:T(8,128)(2,1)}, bf16[128,1024]{1,0:T(8,128)(2,1)S(1)}, u32[]{:S(2)}, u32[]{:S(2)}) collective-permute-start(bf16[128,1024]{1,0:T(8,128)(2,1)} %get-tuple-element.23.refs_0_), channel_id=1, source_target_pairs={{0,4},{1,5},{2,6},{3,7},{4,0},{5,1},{6,2},{7,3},{8,12},{9,13},{10,... | collective-permute-start | bytes 786440 | tf_op jit(solution)/shard_map/ppermute | solution.py:417
  42.8 14.9 %collective-permute-start.1 = (bf16[128,1024]{1,0:T(8,128)(2,1)}, bf16[128,1024]{1,0:T(8,128)(2,1)}, u32[]{:S(2)}, u32[]{:S(2)}) collective-permute-start(bf16[128,1024]{1,0:T(8,128)(2,1)} %get-tuple-element.23.refs_0_), channel_id=1, source_target_pairs={{0,2},{1,3},{2,4},{3,5},{4,6},{5,7},{6,0},{7,1},{8,10},{9,11},{10,... | collective-permute-start | bytes 786440 | tf_op jit(solution)/shard_map/ppermute | solution.py:416
  47.1 16.1 %collective-permute-start.5 = (bf16[128,1024]{1,0:T(8,128)(2,1)S(1)}, bf16[128,1024]{1,0:T(8,128)(2,1)}, u32[]{:S(2)}, u32[]{:S(2)}) collective-permute-start(bf16[128,1024]{1,0:T(8,128)(2,1)S(1)} %collective-permute-done.4.refs_4_), channel_id=1, source_target_pairs={{0,2},{1,3},{2,4},{3,5},{4,6},{5,7},{6,0},{7,1},{8,10},{9,11},{10,... | collective-permute-start | bytes 786440 | tf_op jit(solution)/shard_map/ppermute | solution.py:425
  53.9 9.3 %collective-permute-start.7 = (bf16[128,1024]{1,0:T(8,128)(2,1)S(1)}, bf16[128,1024]{1,0:T(8,128)(2,1)}, u32[]{:S(2)}, u32[]{:S(2)}) collective-permute-start(bf16[128,1024]{1,0:T(8,128)(2,1)S(1)} %collective-permute-done.3.refs_3_), channel_id=1, source_target_pairs={{0,1},{1,0},{2,3},{3,2},{4,5},{5,4},{6,7},{7,6},{8,9},{9,8},{10,11... | collective-permute-start | bytes 786440 | tf_op jit(solution)/shard_map/ppermute | solution.py:427
  54.9 12.1 %collective-permute-start.6 = (bf16[128,1024]{1,0:T(8,128)(2,1)S(1)}, bf16[128,1024]{1,0:T(8,128)(2,1)}, u32[]{:S(2)}, u32[]{:S(2)}) collective-permute-start(bf16[128,1024]{1,0:T(8,128)(2,1)S(1)} %collective-permute-done.2.refs_2_), channel_id=1, source_target_pairs={{0,1},{1,0},{2,3},{3,2},{4,5},{5,4},{6,7},{7,6},{8,9},{9,8},{10,11... | collective-permute-start | bytes 786440 | tf_op jit(solution)/shard_map/ppermute | solution.py:426
  67.0 1.0 copy-start.3
  67.9 1.2 copy-start.6
  69.1 6.0 %copy-start.2 = (bf16[2,512,128]{2,1,0:T(8,128)(2,1)S(1)}, bf16[2,512,128]{2,1,0:T(8,128)(2,1)}, u32[]{:S(2)}) copy-start(bf16[2,512,128]{2,1,0:T(8,128)(2,1)} %constant.117.clone.refs_13_) | copy-start | bytes 786436
  69.1 6.0 %copy-start.4 = (bf16[128,1024]{1,0:T(8,128)(2,1)S(1)}, bf16[128,1024]{1,0:T(8,128)(2,1)}, u32[]{:S(2)}) copy-start(bf16[128,1024]{1,0:T(8,128)(2,1)} %get-tuple-element.23.refs_0_) | copy-start | bytes 786436
  69.2 6.0 %copy-start.5 = (f32[60,1024]{1,0:T(8,128)S(1)}, f32[60,1024]{1,0:T(8,128)}, u32[]{:S(2)}) copy-start(f32[60,1024]{1,0:T(8,128)} %get-tuple-element.21.refs_12_.w_ref) | copy-start | bytes 737284
  69.2 6.0 %copy-start.7 = (bf16[256,384]{1,0:T(8,128)(2,1)S(1)}, bf16[256,384]{1,0:T(8,128)(2,1)}, u32[]{:S(2)}) copy-start(bf16[256,384]{1,0:T(8,128)(2,1)} %constant.114.clone.refs_11_) | copy-start | bytes 589828
  81.5 11.6 %collective-permute-start.9 = (f32[64,256]{1,0:T(8,128)S(1)}, f32[64,256]{1,0:T(8,128)S(1)}, u32[]{:S(2)}, u32[]{:S(2)}) collective-permute-start(f32[64,256]{1,0:T(8,128)S(1)} %get-tuple-element.28), channel_id=1, source_target_pairs={{0,8},{8,16},{16,24},{24,32},{32,40},{40,48},{48,56},{56,64},{64,7... | collective-permute-start | bytes 196616 | tf_op jit(solution)/shard_map/ppermute | solution.py:518
  81.6 11.5 %collective-permute-start.10 = (f32[64,256]{1,0:T(8,128)S(1)}, f32[64,256]{1,0:T(8,128)S(1)}, u32[]{:S(2)}, u32[]{:S(2)}) collective-permute-start(f32[64,256]{1,0:T(8,128)S(1)} %get-tuple-element.29), channel_id=1, source_target_pairs={{0,120},{8,0},{16,8},{24,16},{32,24},{40,32},{48,40},{56,48},{64,5... | collective-permute-start | bytes 196616 | tf_op jit(solution)/shard_map/ppermute | solution.py:517
  87.0 6.2 %copy-start = (f32[60,1024]{1,0:T(8,128)S(1)}, f32[60,1024]{1,0:T(8,128)}, u32[]{:S(2)}) copy-start(f32[60,1024]{1,0:T(8,128)} %res_ref.5) | copy-start | bytes 737284
  87.0 6.2 %copy-start.1 = (f32[64,1024]{1,0:T(8,128)S(1)}, f32[64,1024]{1,0:T(8,128)}, u32[]{:S(2)}) copy-start(f32[64,1024]{1,0:T(8,128)} %inv_ref.5) | copy-start | bytes 786436
  87.0 6.2 %copy-start.8 = (bf16[2,384,128]{2,1,0:T(8,128)(2,1)S(1)}, bf16[2,384,128]{2,1,0:T(8,128)(2,1)}, u32[]{:S(2)}) copy-start(bf16[2,384,128]{2,1,0:T(8,128)(2,1)} %constant.115.clone.own_ref) | copy-start | bytes 589828
  87.0 6.2 %copy-start.9 = (bf16[256,128]{1,0:T(8,128)(2,1)S(1)}, bf16[256,128]{1,0:T(8,128)(2,1)}, u32[]{:S(2)}) copy-start(bf16[256,128]{1,0:T(8,128)(2,1)} %constant.116.clone.near_ref) | copy-start | bytes 196612
  87.0 6.2 %copy-start.12 = (f32[1,128]{1,0:T(1,128)S(1)}, f32[1,128]{1,0:T(1,128)}, u32[]{:S(2)}) copy-start(f32[1,128]{1,0:T(1,128)} %constant.118.clone.count_ref) | copy-start | bytes 1540
  95.9 5.8 %collective-permute-start.14 = (bf16[64,1024]{1,0:T(8,128)(2,1)S(1)}, bf16[64,1024]{1,0:T(8,128)(2,1)S(1)}, u32[]{:S(2)}, u32[]{:S(2)}) collective-permute-start(bf16[64,1024]{1,0:T(8,128)(2,1)S(1)} %get-tuple-element.31.refs_0_), channel_id=1, source_target_pairs={{0,1},{1,0},{2,3},{3,2},{4,5},{5,4},{6,7},{7,6},{8,9},{9,8},{10,11... | collective-permute-start | bytes 393224 | tf_op jit(solution)/shard_map/ppermute | solution.py:415
  97.0 7.8 %collective-permute-start.13 = (bf16[64,1024]{1,0:T(8,128)(2,1)S(1)}, bf16[64,1024]{1,0:T(8,128)(2,1)S(1)}, u32[]{:S(2)}, u32[]{:S(2)}) collective-permute-start(bf16[64,1024]{1,0:T(8,128)(2,1)S(1)} %get-tuple-element.31.refs_0_), channel_id=1, source_target_pairs={{0,6},{1,7},{2,0},{3,1},{4,2},{5,3},{6,4},{7,5},{8,14},{9,15},{10,... | collective-permute-start | bytes 393224 | tf_op jit(solution)/shard_map/ppermute | solution.py:418
  100.8 6.6 %collective-permute-start.12 = (bf16[64,1024]{1,0:T(8,128)(2,1)S(1)}, bf16[64,1024]{1,0:T(8,128)(2,1)S(1)}, u32[]{:S(2)}, u32[]{:S(2)}) collective-permute-start(bf16[64,1024]{1,0:T(8,128)(2,1)S(1)} %get-tuple-element.31.refs_0_), channel_id=1, source_target_pairs={{0,4},{1,5},{2,6},{3,7},{4,0},{5,1},{6,2},{7,3},{8,12},{9,13},{10,... | collective-permute-start | bytes 393224 | tf_op jit(solution)/shard_map/ppermute | solution.py:417
  100.8 7.6 %collective-permute-start.11 = (bf16[64,1024]{1,0:T(8,128)(2,1)S(1)}, bf16[64,1024]{1,0:T(8,128)(2,1)S(1)}, u32[]{:S(2)}, u32[]{:S(2)}) collective-permute-start(bf16[64,1024]{1,0:T(8,128)(2,1)S(1)} %get-tuple-element.31.refs_0_), channel_id=1, source_target_pairs={{0,2},{1,3},{2,4},{3,5},{4,6},{5,7},{6,0},{7,1},{8,10},{9,11},{10,... | collective-permute-start | bytes 393224 | tf_op jit(solution)/shard_map/ppermute | solution.py:416
  101.7 8.1 %collective-permute-start.15 = (bf16[64,1024]{1,0:T(8,128)(2,1)S(1)}, bf16[64,1024]{1,0:T(8,128)(2,1)S(1)}, u32[]{:S(2)}, u32[]{:S(2)}) collective-permute-start(bf16[64,1024]{1,0:T(8,128)(2,1)S(1)} %collective-permute-done.14.refs_4_), channel_id=1, source_target_pairs={{0,2},{1,3},{2,4},{3,5},{4,6},{5,7},{6,0},{7,1},{8,10},{9,11},{10,... | collective-permute-start | bytes 393224 | tf_op jit(solution)/shard_map/ppermute | solution.py:425
  104.7 5.1 %collective-permute-start.17 = (bf16[64,1024]{1,0:T(8,128)(2,1)S(1)}, bf16[64,1024]{1,0:T(8,128)(2,1)S(1)}, u32[]{:S(2)}, u32[]{:S(2)}) collective-permute-start(bf16[64,1024]{1,0:T(8,128)(2,1)S(1)} %collective-permute-done.13.refs_3_), channel_id=1, source_target_pairs={{0,1},{1,0},{2,3},{3,2},{4,5},{5,4},{6,7},{7,6},{8,9},{9,8},{10,11... | collective-permute-start | bytes 393224 | tf_op jit(solution)/shard_map/ppermute | solution.py:427
  107.4 5.0 %collective-permute-start.16 = (bf16[64,1024]{1,0:T(8,128)(2,1)S(1)}, bf16[64,1024]{1,0:T(8,128)(2,1)S(1)}, u32[]{:S(2)}, u32[]{:S(2)}) collective-permute-start(bf16[64,1024]{1,0:T(8,128)(2,1)S(1)} %collective-permute-done.12.refs_2_), channel_id=1, source_target_pairs={{0,1},{1,0},{2,3},{3,2},{4,5},{5,4},{6,7},{7,6},{8,9},{9,8},{10,11... | collective-permute-start | bytes 393224 | tf_op jit(solution)/shard_map/ppermute | solution.py:426
  118.3 11.7 %collective-permute-start.18 = (f32[64,256]{1,0:T(8,128)S(1)}, f32[64,256]{1,0:T(8,128)S(1)}, u32[]{:S(2)}, u32[]{:S(2)}) collective-permute-start(f32[64,256]{1,0:T(8,128)S(1)} %get-tuple-element.34), channel_id=1, source_target_pairs={{0,8},{8,16},{16,24},{24,32},{32,40},{40,48},{48,56},{56,64},{64,7... | collective-permute-start | bytes 196616 | tf_op jit(solution)/shard_map/ppermute | solution.py:518
  118.4 11.7 %collective-permute-start.19 = (f32[64,256]{1,0:T(8,128)S(1)}, f32[64,256]{1,0:T(8,128)S(1)}, u32[]{:S(2)}, u32[]{:S(2)}) collective-permute-start(f32[64,256]{1,0:T(8,128)S(1)} %get-tuple-element.35), channel_id=1, source_target_pairs={{0,120},{8,0},{16,8},{24,16},{32,24},{40,32},{48,40},{56,48},{64,5... | collective-permute-start | bytes 196616 | tf_op jit(solution)/shard_map/ppermute | solution.py:517
